TPU v7x, 128 devices: a whole 4x4x4 slice. The times are simulated.
128 devices in a mesh: req: 4 (over y), exp: 32 (over z, x, core).
Axes of the slice: x: 4, y: 4, z: 4, core: 2. Of those that a mesh axis runs over, the one named last changes fastest.
Arguments:
- residual: bfloat16 [8192, 2048], P(('req', 'exp')), may hold values from -3 to 3
- q_proj: bfloat16 [8192, 4096], P(('req', 'exp')), may hold values from -6 to 6
- kv_proj: bfloat16 [8192, 1024], P(('req', 'exp')), may hold values from -6 to 6
- q_gain: float32 [128], replicated, may hold values from 0.6 to 8
- k_gain: float32 [128], replicated, may hold values from 0.5 to 1.5
- cache_k: bfloat16 [128, 1024, 512], P(('req', 'exp')), may hold values from -21 to 21
- cache_v: bfloat16 [128, 1024, 512], P(('req', 'exp')), may hold values from -6 to 6
- cache_len: int32 [128], P(('req', 'exp')), may hold values from 8 to 960, as said below
- parents: int32 [128, 64], P(('req', 'exp')), may hold values from -1 to 62, as said below
- accepted_leaf: int32 [128], P(('req', 'exp')), may hold values from 0 to 63
- o_weight: bfloat16 [4096, 2048], P(None, 'req'), may hold values from -0.09375 to 0.09375
- post_gain: float32 [2048], replicated, may hold values from 0.1 to 1.9
- routes: int32 [8192, 8], P(('req', 'exp')), may hold values from 0 to 127, all different within a row; in each aligned block of 64 rows (0 to 63, 64 to 127, ...) at most 8 rows name the same one
- route_gates: float32 [8192, 8], P(('req', 'exp')), may hold values from 0.02 to 1
- w_gate: bfloat16 [128, 2048, 768], P(('req', 'exp')), may hold values from -0.125 to 0.125
- w_up: bfloat16 [128, 2048, 768], P(('req', 'exp')), may hold values from -0.125 to 0.125
- w_down: bfloat16 [128, 768, 2048], P(('req', 'exp')), may hold values from -0.21875 to 0.21875
Outputs:
- hidden_out: bfloat16 [8192, 2048], P(('req', 'exp'))
- new_cache_k: bfloat16 [128, 1024, 512], P(('req', 'exp'))
- new_cache_v: bfloat16 [128, 1024, 512], P(('req', 'exp'))
Inputs may be any that keep to these rules, and one draw needn't show every extreme that they name: `cache_len`: some request has exactly 960 cached tokens. parents[r, d] < d; -1 means the draft follows the cached tokens. `routes`: among the rows of one device no expert is named more than 8 times, a bound that some block reaches.
All inputs are finite; a program needn't handle non-finite values.
Results may differ from a plain program's by a relative error of at most 0.015.
Values may be sent and summed in bfloat16 or wider, within the bound.
No kernel may reach another device: no remote copies, remote signals or barrier semaphores. Data moves between devices by JAX's collectives and lax.ppermute only.
A program may use at most 128 MiB of HBM per device.

v0:
```python
import functools

import jax
import jax.numpy as jnp
import numpy as np
from jax import lax
from jax.experimental import pallas as pl
from jax.experimental.pallas import tpu as pltpu
from jax.sharding import PartitionSpec as P


HEADS = 32
KV_HEADS = 4
WINDOW = 512
SINKS = 4

ROPE_BASE = 1000000.0
NORM_EPS = 1e-06
MASKED = -1e30

F32 = jnp.float32
BF16 = jnp.bfloat16


def matmul(a, b):
    return jnp.dot(a, b, preferred_element_type=F32)


def contract(a, b, dims_a, dims_b):
    return lax.dot_general(a, b, (((dims_a,), (dims_b,)), ((), ())), preferred_element_type=F32)


def iota(shape, axis):
    return lax.broadcasted_iota(jnp.int32, shape, axis)


def tables(length, leaf, parents_ref, freq_ref, span, slots, patch):
    draft = parents_ref.shape[1]
    width = freq_ref.shape[1]
    child = iota((draft, draft), 1)
    node = iota((draft, draft), 0)
    eye = (child == node).astype(F32)
    links = (eye + (parents_ref[...] == node).astype(F32)).astype(BF16)
    for _ in range((draft - 1).bit_length()):
        links = jnp.minimum(matmul(links, links), 1.0).astype(BF16)
    closure = contract(links, eye.astype(BF16), 0, 0)
    depth = jnp.sum(closure, axis=1, keepdims=True) - 1.0
    angle = (length.astype(F32) + depth) * freq_ref[...]
    sine = jnp.sin(angle)
    sine = jnp.where(iota((draft, width), 1) < width // 2, -sine, sine)
    head = iota((draft, width - draft), 1)
    first = jnp.minimum(jnp.maximum(length - WINDOW, 0) // 16 * 16, slots - span)
    seen = (head < SINKS) & (head < length) & (head < first)
    tree = jnp.concatenate(
        [jnp.where(closure > 0.5, 0.0, MASKED), jnp.where(seen, 0.0, MASKED)], axis=1
    )
    chosen = (iota((8, draft), 1) == leaf).astype(BF16)
    accepted = matmul(chosen, closure.astype(BF16))[:1]
    depths = contract(jnp.ones((8, draft), BF16), closure.astype(BF16), 1, 1)[:1] - 1.0
    row = iota((patch, draft), 0) + patch_start(length, slots, patch) - length
    place = ((row == depths.astype(jnp.int32)) & (accepted > 0.5)).astype(BF16)
    return jnp.cos(angle), sine, tree, place


def patch_start(length, slots, patch):
    return jnp.minimum(length // 16 * 16, slots - patch)


def attention_kernel(opening, span, *refs):
    length_ref, leaf_ref, q_gain_ref, k_gain_ref, q_ref, k_ref, v_ref, cache_k_ref, cache_v_ref = refs[:9]
    refs = refs[9:]
    if opening:
        parents_ref, freq_ref, out_ref, key_ref, cos_ref, sin_ref, tree_ref, place_ref = refs
    else:
        cos_ref, sin_ref, tree_ref, out_ref, key_ref = refs
    draft = k_ref.shape[0]
    width = k_ref.shape[1]
    slots = cache_k_ref.shape[0]
    group = q_ref.shape[1] // width
    length = length_ref[0]

    if opening:

        @pl.when(pl.program_id(0) == 0)
        def _():
            made = tables(
                length, leaf_ref[0], parents_ref, freq_ref, span, slots, place_ref.shape[0]
            )
            for ref, table in zip((cos_ref, sin_ref, tree_ref, place_ref), made):
                ref[...] = table

    cosine = cos_ref[...]
    sine = sin_ref[...]

    def turned(x, gain):
        x = x * lax.rsqrt(jnp.mean(x * x, axis=-1, keepdims=True) + NORM_EPS) * gain
        return x, pltpu.roll(x, width // 2, axis=1)

    k_new, k_swapped = turned(k_ref[...].astype(F32), k_gain_ref[...])
    k_new = (k_new * cosine + k_swapped * sine).astype(BF16)
    key_ref[...] = k_new
    queries = q_ref[...].astype(F32)
    queries = jnp.concatenate(
        [queries[:, h * width : (h + 1) * width] for h in range(group)], axis=0
    )
    queries, q_swapped = turned(queries, q_gain_ref[...])
    shape = (group, draft, width)
    queries = (
        queries.reshape(shape) * cosine[None] + q_swapped.reshape(shape) * sine[None]
    ).reshape(group * draft, width).astype(BF16)

    first = jnp.minimum(jnp.maximum(length - WINDOW, 0) // 16 * 16, slots - span)
    first = pl.multiple_of(first, 16)
    pad = jnp.zeros((width - draft - 16, width), BF16)
    keys = cache_k_ref[pl.ds(first, span), :]
    values = cache_v_ref[pl.ds(first, span), :]
    own_keys = jnp.concatenate([k_new, cache_k_ref[:16, :], pad], axis=0)
    own_values = jnp.concatenate([v_ref[...], cache_v_ref[:16, :], pad], axis=0)
    slot = iota((1, span), 1) + first
    seen = (slot < length) & ((slot < SINKS) | (slot >= length - WINDOW))
    far = contract(queries, keys, 1, 1) + jnp.where(seen, 0.0, MASKED)
    near = contract(queries, own_keys, 1, 1).reshape(shape) + tree_ref[...][None]
    near = near.reshape(group * draft, width)
    top = jnp.maximum(
        jnp.max(far, axis=-1, keepdims=True), jnp.max(near, axis=-1, keepdims=True)
    )
    scale = float(width) ** -0.5 * float(np.log2(np.e))
    far = jnp.exp2((far - top) * scale)
    near = jnp.exp2((near - top) * scale)
    total = jnp.sum(far, axis=-1, keepdims=True) + jnp.sum(near, axis=-1, keepdims=True)
    mixed = matmul(far.astype(BF16), values) + matmul(near.astype(BF16), own_values)
    mixed = (mixed / total).astype(BF16)
    for h in range(group):
        out_ref[:, h * width : (h + 1) * width] = mixed[h * draft : (h + 1) * draft]


def attention(length, leaf, parents, q_gain, k_gain, q_proj, kv_proj, cache_k, cache_v, at, made):
    draft = q_proj.shape[0]
    width = q_gain.shape[0]
    slots = cache_k.shape[0]
    span = min(slots, WINDOW + 128)
    per_group = HEADS // KV_HEADS * width
    groups = KV_HEADS // 2
    base = at * groups
    smem = pl.BlockSpec(memory_space=pltpu.SMEM)
    whole = lambda shape: pl.BlockSpec(shape, lambda g: (0, 0))
    table = jax.ShapeDtypeStruct((draft, width), F32)
    patch = draft + 16
    tables_shape = [table] * 3 + [jax.ShapeDtypeStruct((patch, draft), BF16)]
    in_specs = [
        smem,
        smem,
        whole((1, width)),
        whole((1, width)),
        pl.BlockSpec((draft, per_group), lambda g: (0, g + base)),
        pl.BlockSpec((draft, width), lambda g: (0, g + base)),
        pl.BlockSpec((draft, width), lambda g: (0, g + base + KV_HEADS)),
        pl.BlockSpec((slots, width), lambda g: (0, g + base)),
        pl.BlockSpec((slots, width), lambda g: (0, g + base)),
    ]
    out_specs = [
        pl.BlockSpec((draft, per_group), lambda g: (0, g)),
        pl.BlockSpec((draft, width), lambda g: (0, g)),
    ]
    out_shape = [
        jax.ShapeDtypeStruct((draft, per_group * groups), BF16),
        jax.ShapeDtypeStruct((draft, width * groups), BF16),
    ]
    operands = [length, leaf, q_gain[None], k_gain[None], q_proj, kv_proj, kv_proj, cache_k, cache_v]
    if made is None:
        half = width // 2
        freq = ROPE_BASE ** (-(np.arange(half) * 2.0) / width)
        freq = jnp.asarray(np.concatenate([freq, freq])[None, :], F32)
        operands += [parents, freq]
        in_specs += [whole((1, draft)), whole((1, width))]
        out_specs += [whole(t.shape) for t in tables_shape]
        out_shape += tables_shape
    else:
        operands += made[:3]
        in_specs += [whole(t.shape) for t in made[:3]]
    return pl.pallas_call(
        functools.partial(attention_kernel, made is None, span),
        grid=(groups,),
        in_specs=in_specs,
        out_specs=out_specs,
        out_shape=out_shape,
        cost_estimate=pl.CostEstimate(
            flops=2 * HEADS * draft * (span + width) * width,
            bytes_accessed=2 << 20,
            transcendentals=HEADS // 2 * draft * (span + width),
        ),
    )(*operands)


def append_kernel(length_ref, place_ref, cache_ref, *rest):
    new_ref = rest[-1]
    patch = place_ref.shape[0]
    slots = cache_ref.shape[0]
    at = pl.multiple_of(patch_start(length_ref[0], slots, patch), 16)
    place = place_ref[...]
    taken = jnp.sum(place.astype(F32), axis=1, keepdims=True) > 0.5
    rows = pl.ds(at, patch)
    fresh = rest[0][...]
    if len(rest) > 2:
        fresh = jnp.where(pl.program_id(0) == 0, fresh, rest[1][...])
    new_ref[...] = cache_ref[...]
    put = matmul(place, fresh).astype(BF16)
    new_ref[rows, :] = jnp.where(taken, put, cache_ref[rows, :])


def append(length, place, cache, fresh):
    slots, width = cache.shape
    draft = place.shape[1]
    cols = width // 2
    whole = lambda x: pl.BlockSpec(x.shape, lambda g: (0, 0))
    cache_spec = pl.BlockSpec((slots, cols), lambda g: (0, g))
    last = [pl.BlockSpec((draft, cols), lambda g: (0, g + 2))]
    return pl.pallas_call(
        append_kernel,
        grid=(2,),
        in_specs=[pl.BlockSpec(memory_space=pltpu.SMEM), whole(place), cache_spec]
        + (last if len(fresh) == 1 else [whole(x) for x in fresh]),
        out_specs=cache_spec,
        out_shape=jax.ShapeDtypeStruct(cache.shape, BF16),
        cost_estimate=pl.CostEstimate(
            flops=4 * place.shape[0] * draft * cols,
            bytes_accessed=4 * slots * width,
            transcendentals=0,
        ),
    )(length, place, cache, *fresh)


def second_kernel(x_ref, gate_ref, up_ref, down_ref, gate_in, up_in, hidden_out, sent_out):
    x = x_ref[...]
    gate = matmul(x, gate_ref[...]) + gate_in[...]
    up = matmul(x, up_ref[...]) + up_in[...]
    hidden = (gate / (1.0 + jnp.exp(-gate)) * up).astype(BF16)
    hidden_out[...] = hidden
    sent_out[...] = matmul(hidden, down_ref[...]).astype(BF16)


def second_half(x, w_gate, w_up, w_down, gate, up):
    count, cols = x.shape
    width = w_gate.shape[1]
    rows = 128
    once = pl.Buffered(1)
    by_rows = lambda n: pl.BlockSpec((rows, n), lambda i: (i, 0))
    part = pl.BlockSpec((cols, width), lambda i: (1, 0), pipeline_mode=once)
    down = pl.BlockSpec((width, cols), lambda i: (0, 0), pipeline_mode=once)
    return pl.pallas_call(
        second_kernel,
        grid=(count // rows,),
        in_specs=[by_rows(cols), part, part, down, by_rows(width), by_rows(width)],
        out_specs=[by_rows(width), by_rows(cols)],
        out_shape=[
            jax.ShapeDtypeStruct((count, width), BF16),
            jax.ShapeDtypeStruct((count, cols), BF16),
        ],
        name="experts_second",
        cost_estimate=pl.CostEstimate(
            flops=6 * count * cols * width, bytes_accessed=16 << 20, transcendentals=count * width
        ),
    )(x, w_gate, w_up, w_down, gate, up)


def down_kernel(hidden_ref, down_ref, out_ref):
    out_ref[...] = matmul(hidden_ref[...], down_ref[...]).astype(BF16)


def last_columns(hidden, w_down, cols):
    count, width = hidden.shape
    rows = 256
    return pl.pallas_call(
        down_kernel,
        grid=(count // rows,),
        in_specs=[
            pl.BlockSpec((rows, width), lambda i: (i, 0)),
            pl.BlockSpec((width, cols), lambda i: (0, 1), pipeline_mode=pl.Buffered(1)),
        ],
        out_specs=pl.BlockSpec((rows, cols), lambda i: (i, 0)),
        out_shape=jax.ShapeDtypeStruct((count, cols), BF16),
        name="experts_third",
        cost_estimate=pl.CostEstimate(
            flops=2 * count * cols * width, bytes_accessed=5 << 20, transcendentals=0
        ),
    )(hidden, w_down)


def slot_table(routes, expert_count, capacity):
    tokens = routes.shape[0]
    onehot = routes[:, :, None] == jnp.arange(expert_count, dtype=jnp.int32)[None, None, :]
    used = jnp.any(onehot, axis=1).astype(BF16)
    earlier = jnp.asarray(np.tril(np.ones((tokens, tokens)), -1), BF16)
    rank = matmul(earlier, used)
    rank = jnp.sum(jnp.where(onehot, rank[:, None, :], 0.0), axis=2).astype(jnp.int32)
    return routes * capacity + rank


def gather_plan(slots, gates, slot_count):
    index = jnp.arange(slot_count, dtype=jnp.int32)
    slots_t = slots.T
    pick = index[:, None] == slots_t[0][None, :]
    mix = jnp.where(index[None, :] == slots[:, :1], gates[:, :1], 0.0)
    for k in range(1, slots.shape[1]):
        pick = pick | (index[:, None] == slots_t[k][None, :])
        mix = jnp.where(index[None, :] == slots[:, k : k + 1], gates[:, k : k + 1], mix)
    high = lax.reduce_precision(mix, 8, 7)
    return pick.astype(BF16), jnp.concatenate([high, mix - high], axis=0).astype(BF16)


def shift(x, by, size):
    return lax.ppermute(x, "req", [(i, (i + by) % size) for i in range(size)])


def body(
    residual,
    q_proj,
    kv_proj,
    q_gain,
    k_gain,
    cache_k,
    cache_v,
    cache_len,
    parents,
    accepted_leaf,
    o_weight,
    post_gain,
    routes,
    route_gates,
    w_gate,
    w_up,
    w_down,
):
    tok_rows, model_width = residual.shape
    req_size = lax.axis_size("req")
    exp_size = lax.axis_size("exp")
    expert_count = req_size * exp_size
    top_count = routes.shape[1]
    capacity = max(2, 2 * tok_rows * top_count // expert_count)
    slot_count = expert_count * capacity
    half = model_width // 2

    attend = functools.partial(
        attention,
        cache_len,
        accepted_leaf,
        parents,
        q_gain,
        k_gain,
        q_proj,
        kv_proj,
        cache_k[0],
        cache_v[0],
    )
    left, left_keys, *made = attend(0, None)
    right, right_keys = attend(1, made)
    new_keys = append(cache_len, made[3], cache_k[0], [left_keys, right_keys])
    new_values = append(cache_len, made[3], cache_v[0], [kv_proj])
    slots = slot_table(routes, expert_count, capacity)
    pick, mix = gather_plan(slots, route_gates, slot_count)

    inner = left.shape[1]
    up_left, down_left = shift(left, -1, req_size), shift(left, 1, req_size)
    up_right, down_right = shift(right, -1, req_size), shift(right, 1, req_size)
    far_left = shift(up_left, -1, req_size)
    far_right = shift(down_right, 1, req_size)

    def project(a, b):
        return (matmul(a, o_weight[:inner]) + matmul(b, o_weight[inner:])).astype(BF16)

    own = project(left, right)
    near_up = project(up_left, up_right)
    near_down = project(down_left, down_right)
    from_up = shift(near_up, 1, req_size)
    from_down = shift(near_down, -1, req_size)
    from_far = shift(project(far_left, far_right), 2, req_size)
    pieces = [own, from_down, from_far, from_up]
    at = lax.axis_index("req").astype(jnp.int32)
    columns = []
    for j in range(req_size):
        step = lax.rem(j - at + req_size, req_size)
        column = pieces[0]
        for s in range(1, req_size):
            column = jnp.where(step == s, pieces[s], column)
        columns.append(column)
    projected = jnp.concatenate(columns, axis=1).astype(F32)
    middle = (residual.astype(F32) + projected).astype(BF16)
    middle32 = middle.astype(F32)
    power = jnp.mean(middle32 * middle32, axis=-1, keepdims=True)
    normed = (middle32 * lax.rsqrt(power + NORM_EPS) * post_gain).astype(BF16)

    def swap(x):
        return lax.all_to_all(
            x.reshape(expert_count, capacity, -1),
            ("req", "exp"),
            split_axis=0,
            concat_axis=0,
            tiled=True,
        ).reshape(slot_count, -1)

    parts = (slice(0, half), slice(half, model_width))
    arrived = [swap(matmul(pick, normed[:, part]).astype(BF16)) for part in parts]
    gate = matmul(arrived[0], w_gate[0, parts[0]])
    up = matmul(arrived[0], w_up[0, parts[0]])
    hidden, sent = second_half(arrived[1], w_gate[0], w_up[0], w_down[0], gate, up)
    sent = [sent, last_columns(hidden, w_down[0], half)]
    outs = []
    for part, out in zip(parts, sent):
        mixture = matmul(mix, swap(out))
        outs.append(middle32[:, part] + (mixture[:tok_rows] + mixture[tok_rows:]))
    hidden_out = jnp.concatenate(outs, axis=1).astype(BF16)
    return (hidden_out, new_keys[None], new_values[None])


def solution(mesh):
    placed = (
        P(("req", "exp"), None),
        P(("req", "exp"), None),
        P(("req", "exp"), None),
        P(),
        P(),
        P(("req", "exp"), None, None),
        P(("req", "exp"), None, None),
        P(("req", "exp")),
        P(("req", "exp"), None),
        P(("req", "exp")),
        P(None, "req"),
        P(),
        P(("req", "exp"), None),
        P(("req", "exp"), None),
        P(("req", "exp"), None, None),
        P(("req", "exp"), None, None),
        P(("req", "exp"), None, None),
    )
    return jax.shard_map(
        body,
        mesh=mesh,
        in_specs=placed,
        out_specs=(
            P(("req", "exp"), None),
            P(("req", "exp"), None, None),
            P(("req", "exp"), None, None),
        ),
        check_vma=False,
    )
```

profile of v0, /device:TPU:1, one launch (start us, length us, event | category | flops | bytes accessed | tf_op | source)
XLA Modules:
  0.0 215.8 jit_solution(7471826722818318444)
XLA Ops:
  1.9 6.1 %shard_map.202 = (bf16[64,2048]{1,0:T(8,128)(2,1)}, bf16[64,256]{1,0:T(8,128)(2,1)}, f32[64,128]{1,0:T(8,128)}, f32[64,128]{1,0:T(8,128)}, f32[64,128]{1,0:T(8,128)}, /*index=5*/bf16[80,64]{1,0:T(8,128)(2,1)}) custom-call(s32[1]{0:T(128)S(6)} %copy.31.refs_0_.length_ref, s32[1]{0:T(128)S(6)} %copy.32.refs_1_, f32[1,128]{1,0:T(1,128)} %bitcast.105, ...), custom_call_target="tpu_custom_call" | custom-call | flops 402653184 | bytes 2097152 | tf_op jit(solution)/shard_map/pallas_call | solution.py:181
  8.0 3.6 %collective-permute-start = (bf16[64,2048]{1,0:T(8,128)(2,1)}, bf16[64,2048]{1,0:T(8,128)(2,1)S(1)}, u32[]{:S(2)}, u32[]{:S(2)}) collective-permute-start(bf16[64,2048]{1,0:T(8,128)(2,1)} %get-tuple-element.13), channel_id=1, source_target_pairs={{0,96},{32,0},{64,32},{96,64},{1,97},{33,1},{65,33},{97,65},{2,98}... | collective-permute-start | bytes 786440 | tf_op jit(solution)/shard_map/ppermute | solution.py:312
  11.6 4.9 %shard_map.203 = (bf16[64,2048]{1,0:T(8,128)(2,1)}, bf16[64,256]{1,0:T(8,128)(2,1)}) custom-call(s32[1]{0:T(128)S(6)} %copy.31.refs_0_.length_ref, s32[1]{0:T(128)S(6)} %copy.32.refs_1_, f32[1,128]{1,0:T(1,128)} %bitcast.106, f32[1,128]{1,0:T(1,128)} %bitcast.108, bf16[64,4096]{1,0:T(8,128)(2,1)} %refs_4_.3, bf16[64,1024]{1,0:T(8,128)(2,1)} %rest_0_.1, ...), custom_call_target="tpu_custom_call" | custom-call | flops 402653184 | bytes 2097152 | tf_op jit(solution)/shard_map/pallas_call | solution.py:181
  16.6 0.1 collective-permute-start.4
  16.7 2.7 %collective-permute-start.1 = (bf16[64,2048]{1,0:T(8,128)(2,1)}, bf16[64,2048]{1,0:T(8,128)(2,1)S(1)}, u32[]{:S(2)}, u32[]{:S(2)}) collective-permute-start(bf16[64,2048]{1,0:T(8,128)(2,1)} %get-tuple-element.17), channel_id=1, source_target_pairs={{0,96},{32,0},{64,32},{96,64},{1,97},{33,1},{65,33},{97,65},{2,98}... | collective-permute-start | bytes 786440 | tf_op jit(solution)/shard_map/ppermute | solution.py:312
  19.4 2.2 fusion.12
  21.6 0.1 copy.29
  21.7 0.2 fusion.65
  21.9 0.1 fusion.72
  22.0 0.2 select_reduce_fusion
  22.3 2.2 %fusion.40 = bf16[64,512]{1,0:T(8,128)(2,1)S(1)} fusion(f32[64,512]{1,0:T(8,128)S(1)} %fusion.12, bf16[64,2048]{1,0:T(8,128)(2,1)S(1)} %copy-done.7, bf16[4096,512]{1,0:T(8,128)(2,1)} %param.29), kind=kOutput, calls=%fused_computation.34 | convolution fusion | flops 134283264 | bytes 2555904 | tf_op jit(solution)/shard_map/dot_general | solution.py:26
  24.5 1.6 collective-permute-done.4
  26.2 2.1 fusion.14
  28.3 0.5 fusion.43
  28.7 0.1 collective-permute-start.8
  28.8 1.4 collective-permute-start.5
  30.3 0.5 fusion.18
  30.8 0.5 fusion.49
  31.2 0.1 collective-permute-start.2
  31.3 2.7 %collective-permute-start.3 = (bf16[64,2048]{1,0:T(8,128)(2,1)S(1)}, bf16[64,2048]{1,0:T(8,128)(2,1)S(1)}, u32[]{:S(2)}, u32[]{:S(2)}) collective-permute-start(bf16[64,2048]{1,0:T(8,128)(2,1)S(1)} %collective-permute-done), channel_id=1, source_target_pairs={{0,96},{32,0},{64,32},{96,64},{1,97},{33,1},{65,33},{97,65},{2,98}... | collective-permute-start | bytes 786440 | tf_op jit(solution)/shard_map/ppermute | solution.py:312
  34.0 1.6 collective-permute-done.5
  35.6 0.5 fusion.16
  36.1 1.4 collective-permute-done.3
  37.6 0.5 fusion.46
  38.0 1.8 collective-permute-start.6
  39.9 2.9 %collective-permute-done.6 = bf16[64,512]{1,0:T(8,128)(2,1)S(1)} collective-permute-done((bf16[64,512]{1,0:T(8,128)(2,1)S(1)}, bf16[64,512]{1,0:T(8,128)(2,1)S(1)}, u32[]{:S(2)}, u32[]{:S(2)}) %collective-permute-start.6) | collective-permute-done | bytes 65568 | tf_op jit(solution)/shard_map/ppermute | solution.py:312
  42.8 0.2 fusion.60
  43.0 0.1 multiply_convert_fusion
  43.1 2.2 %convert_bitcast_fusion = bf16[128,8,1024]{2,1,0:T(8,128)(2,1)} fusion(bf16[64,2048]{1,0:T(8,128)(2,1)S(1)} %multiply_convert_fusion, s32[64]{0:T(128)S(1)} %get-tuple-element.50, s32[64]{0:T(128)S(1)} %get-tuple-element.51, s32[64]{0:T(128)S(1)} %get-tuple-element.52, s32[64]{0:T(128)S(1)} %get-tuple-element.53, s32[64]{0:T(128)S(1)} %get-tuple-element.54, ...), kind=kOutput, calls=%fused_computation.8 | convolution fusion | flops 136249344 | bytes 2232320 | tf_op jit(solution)/shard_map/dot_general | solution.py:26
  45.4 14.6 %all-to-all-start.1 = ((bf16[128,8,1024]{2,1,0:T(8,128)(2,1)}), bf16[128,8,1024]{2,1,0:T(8,128)(2,1)S(1)}, u32[]{:S(2)}, u32[]{:S(2)}) async-start(bf16[128,8,1024]{2,1,0:T(8,128)(2,1)} %convert_bitcast_fusion), calls=%async_computation.1 | async-start | bytes 4194304 | tf_op jit(solution)/shard_map/all_to_all | solution.py:393
  59.9 2.2 %convert_bitcast_fusion.1 = bf16[128,8,1024]{2,1,0:T(8,128)(2,1)} fusion(bf16[64,2048]{1,0:T(8,128)(2,1)S(1)} %multiply_convert_fusion, s32[64]{0:T(128)S(1)} %get-tuple-element.50, s32[64]{0:T(128)S(1)} %get-tuple-element.51, s32[64]{0:T(128)S(1)} %get-tuple-element.52, s32[64]{0:T(128)S(1)} %get-tuple-element.53, s32[64]{0:T(128)S(1)} %get-tuple-element.54, ...), kind=kOutput, calls=%fused_computation.9 | convolution fusion | flops 136249344 | bytes 2232320 | tf_op jit(solution)/shard_map/dot_general | solution.py:26
  62.2 28.2 %all-to-all-done.1 = bf16[128,8,1024]{2,1,0:T(8,128)(2,1)S(1)} async-done(((bf16[128,8,1024]{2,1,0:T(8,128)(2,1)}), bf16[128,8,1024]{2,1,0:T(8,128)(2,1)S(1)}, u32[]{:S(2)}, u32[]{:S(2)}) %all-to-all-start.1) | async-done | bytes 2097184 | tf_op jit(solution)/shard_map/all_to_all | solution.py:393
  90.4 5.5 %all-to-all-start = ((bf16[128,8,1024]{2,1,0:T(8,128)(2,1)}), bf16[128,8,1024]{2,1,0:T(8,128)(2,1)}, u32[]{:S(2)}, u32[]{:S(2)}) async-start(bf16[128,8,1024]{2,1,0:T(8,128)(2,1)} %convert_bitcast_fusion.1), calls=%async_computation | async-start | bytes 4194304 | tf_op jit(solution)/shard_map/all_to_all | solution.py:393
  95.9 5.1 %fusion.4.up_in = f32[1024,768]{1,0:T(8,128)} fusion(bf16[128,8,1024]{2,1,0:T(8,128)(2,1)S(1)} %all-to-all-done.1, bf16[1,2048,768]{2,1,0:T(8,128)(2,1)} %param.34), kind=kOutput, calls=%fused_computation.4 | convolution fusion | flops 1610612736 | bytes 6815744 | tf_op jit(solution)/shard_map/dot_general | solution.py:26
  101.0 3.4 %fusion.6.gate_in = f32[1024,768]{1,0:T(8,128)} fusion(bf16[128,8,1024]{2,1,0:T(8,128)(2,1)S(1)} %all-to-all-done.1, bf16[1,2048,768]{2,1,0:T(8,128)(2,1)S(1)} %copy-done.6), kind=kOutput, calls=%fused_computation.6 | convolution fusion | flops 1610612736 | bytes 6815744 | tf_op jit(solution)/shard_map/dot_general | solution.py:26
  104.4 21.7 %all-to-all-done = bf16[128,8,1024]{2,1,0:T(8,128)(2,1)} async-done(((bf16[128,8,1024]{2,1,0:T(8,128)(2,1)}), bf16[128,8,1024]{2,1,0:T(8,128)(2,1)}, u32[]{:S(2)}, u32[]{:S(2)}) %all-to-all-start) | async-done | bytes 2097184 | tf_op jit(solution)/shard_map/all_to_all | solution.py:393
  126.1 12.1 %experts_second.1 = (bf16[1024,768]{1,0:T(8,128)(2,1)}, bf16[1024,1024]{1,0:T(8,128)(2,1)}) custom-call(bf16[1024,1024]{1,0:T(8,128)(2,1)} %bitcast.30.x_ref, bf16[2048,768]{1,0:T(8,128)(2,1)} %bitcast.109, bf16[2048,768]{1,0:T(8,128)(2,1)} %bitcast.110, bf16[768,2048]{1,0:T(8,128)(2,1)} %bitcast.99, f32[1024,768]{1,0:T(8,128)} %fusion.6.gate_in, ...), custom_call_target="tpu_custom_call" | custom-call | flops 4831838208 | bytes 16777216 | tf_op jit(solution)/shard_map/experts_second/pallas_call | solution.py:250
  138.2 5.3 %experts_third.1 = bf16[1024,1024]{1,0:T(8,128)(2,1)} custom-call(bf16[1024,768]{1,0:T(8,128)(2,1)} %get-tuple-element.19.hidden_ref, bf16[768,2048]{1,0:T(8,128)(2,1)} %bitcast.100), custom_call_target="tpu_custom_call" | custom-call | flops 1610612736 | bytes 5242880 | tf_op jit(solution)/shard_map/experts_third/pallas_call | solution.py:273
  143.5 35.9 %all_to_all.20 = bf16[128,8,1024]{2,1,0:T(8,128)(2,1)} all-to-all(bf16[128,8,1024]{2,1,0:T(8,128)(2,1)} %bitcast.98), channel_id=1, replica_groups=mesh['req'=4,'exp'=32] {'req','exp'}, dimensions={0} | all-to-all | bytes 4194304 | tf_op jit(solution)/shard_map/all_to_all | solution.py:393
  179.5 4.4 %all-to-all-start.2 = ((bf16[128,8,1024]{2,1,0:T(8,128)(2,1)}), bf16[128,8,1024]{2,1,0:T(8,128)(2,1)S(1)}, u32[]{:S(2)}, u32[]{:S(2)}) async-start(bf16[128,8,1024]{2,1,0:T(8,128)(2,1)} %bitcast.101), calls=%async_computation.2 | async-start | bytes 4194304 | tf_op jit(solution)/shard_map/all_to_all | solution.py:393
  183.9 2.2 %shard_map.205 = bf16[1024,512]{1,0:T(8,128)(2,1)} custom-call(s32[1]{0:T(128)S(6)} %copy.31.refs_0_.length_ref, bf16[80,64]{1,0:T(8,128)(2,1)} %get-tuple-element.20.place_ref, bf16[1024,512]{1,0:T(8,128)(2,1)} %bitcast.94, bf16[64,1024]{1,0:T(8,128)(2,1)} %rest_0_.1), custom_call_target="tpu_custom_call" | custom-call | flops 5242880 | bytes 2097152 | tf_op jit(solution)/shard_map/pallas_call | solution.py:218
  186.1 2.2 %shard_map.204 = bf16[1024,512]{1,0:T(8,128)(2,1)} custom-call(s32[1]{0:T(128)S(6)} %copy.31.refs_0_.length_ref, bf16[80,64]{1,0:T(8,128)(2,1)} %get-tuple-element.20.place_ref, bf16[1024,512]{1,0:T(8,128)(2,1)} %bitcast.97, bf16[64,256]{1,0:T(8,128)(2,1)} %get-tuple-element.21.rest_0_, bf16[64,256]{1,0:T(8,128)(2,1)} %get-tuple-element.22.rest_1_), custom_call_target="tpu_custom_call" | custom-call | flops 5242880 | bytes 2097152 | tf_op jit(solution)/shard_map/pallas_call | solution.py:218
  188.3 0.4 reduce-precision_convert_fusion
  188.7 2.0 fusion
  190.7 23.7 %all-to-all-done.2 = bf16[128,8,1024]{2,1,0:T(8,128)(2,1)S(1)} async-done(((bf16[128,8,1024]{2,1,0:T(8,128)(2,1)}), bf16[128,8,1024]{2,1,0:T(8,128)(2,1)S(1)}, u32[]{:S(2)}, u32[]{:S(2)}) %all-to-all-start.2) | async-done | bytes 2097184 | tf_op jit(solution)/shard_map/all_to_all | solution.py:393
  214.5 0.4 fusion.2
  214.9 0.1 fusion.64
  215.0 0.7 pad_maximum_fusion.1
  (29 shorter events, 0.2 us)
Async XLA Ops:
  8.0 22.7 %collective-permute-start = (bf16[64,2048]{1,0:T(8,128)(2,1)}, bf16[64,2048]{1,0:T(8,128)(2,1)S(1)}, u32[]{:S(2)}, u32[]{:S(2)}) collective-permute-start(bf16[64,2048]{1,0:T(8,128)(2,1)} %get-tuple-element.13), channel_id=1, source_target_pairs={{0,96},{32,0},{64,32},{96,64},{1,97},{33,1},{65,33},{97,65},{2,98}... | collective-permute-start | bytes 786440 | tf_op jit(solution)/shard_map/ppermute | solution.py:312
  11.6 16.6 %collective-permute-start.7 = (bf16[64,2048]{1,0:T(8,128)(2,1)}, bf16[64,2048]{1,0:T(8,128)(2,1)S(1)}, u32[]{:S(2)}, u32[]{:S(2)}) collective-permute-start(bf16[64,2048]{1,0:T(8,128)(2,1)} %get-tuple-element.13), channel_id=1, source_target_pairs={{0,32},{32,64},{64,96},{96,0},{1,33},{33,65},{65,97},{97,1},{2,34}... | collective-permute-start | bytes 786440 | tf_op jit(solution)/shard_map/ppermute | solution.py:312
  11.6 10.0 %copy-start.2 = (s32[64,8]{0,1:T(8,128)S(1)}, s32[64,8]{0,1:T(8,128)}, u32[]{:S(2)}) copy-start(s32[64,8]{0,1:T(8,128)} %param.31) | copy-start | bytes 6148
  16.6 5.3 %copy-start.1 = (bf16[64,64]{1,0:T(8,128)(2,1)S(1)}, bf16[64,64]{1,0:T(8,128)(2,1)}, u32[]{:S(2)}) copy-start(bf16[64,64]{1,0:T(8,128)(2,1)} %constant.46.clone) | copy-start | bytes 24580
  16.6 5.7 %copy-start.7 = (bf16[64,2048]{1,0:T(8,128)(2,1)S(1)}, bf16[64,2048]{1,0:T(8,128)(2,1)}, u32[]{:S(2)}) copy-start(bf16[64,2048]{1,0:T(8,128)(2,1)} %get-tuple-element.13) | copy-start | bytes 786436
  16.6 9.6 %collective-permute-start.4 = (bf16[64,2048]{1,0:T(8,128)(2,1)}, bf16[64,2048]{1,0:T(8,128)(2,1)S(1)}, u32[]{:S(2)}, u32[]{:S(2)}) collective-permute-start(bf16[64,2048]{1,0:T(8,128)(2,1)} %get-tuple-element.17), channel_id=1, source_target_pairs={{0,32},{32,64},{64,96},{96,0},{1,33},{33,65},{65,97},{97,1},{2,34}... | collective-permute-start | bytes 786440 | tf_op jit(solution)/shard_map/ppermute | solution.py:312
  16.7 13.6 %collective-permute-start.1 = (bf16[64,2048]{1,0:T(8,128)(2,1)}, bf16[64,2048]{1,0:T(8,128)(2,1)S(1)}, u32[]{:S(2)}, u32[]{:S(2)}) collective-permute-start(bf16[64,2048]{1,0:T(8,128)(2,1)} %get-tuple-element.17), channel_id=1, source_target_pairs={{0,96},{32,0},{64,32},{96,64},{1,97},{33,1},{65,33},{97,65},{2,98}... | collective-permute-start | bytes 786440 | tf_op jit(solution)/shard_map/ppermute | solution.py:312
  22.3 5.9 %copy-start.5 = (bf16[4096,512]{1,0:T(8,128)(2,1)S(1)}, bf16[4096,512]{1,0:T(8,128)(2,1)}, u32[]{:S(2)}) copy-start(bf16[4096,512]{1,0:T(8,128)(2,1)} %param.29) | copy-start | bytes 12582916
  28.7 11.1 %collective-permute-start.8 = (bf16[64,512]{1,0:T(8,128)(2,1)S(1)}, bf16[64,512]{1,0:T(8,128)(2,1)S(1)}, u32[]{:S(2)}, u32[]{:S(2)}) collective-permute-start(bf16[64,512]{1,0:T(8,128)(2,1)S(1)} %fusion.43), channel_id=1, source_target_pairs={{0,96},{32,0},{64,32},{96,64},{1,97},{33,1},{65,33},{97,65},{2,98}... | collective-permute-start | bytes 196616 | tf_op jit(solution)/shard_map/ppermute | solution.py:312
  28.8 6.8 %collective-permute-start.5 = (bf16[64,2048]{1,0:T(8,128)(2,1)S(1)}, bf16[64,2048]{1,0:T(8,128)(2,1)S(1)}, u32[]{:S(2)}, u32[]{:S(2)}) collective-permute-start(bf16[64,2048]{1,0:T(8,128)(2,1)S(1)} %collective-permute-done.4), channel_id=1, source_target_pairs={{0,32},{32,64},{64,96},{96,0},{1,33},{33,65},{65,97},{97,1},{2,34}... | collective-permute-start | bytes 786440 | tf_op jit(solution)/shard_map/ppermute | solution.py:312
  31.2 8.6 %collective-permute-start.2 = (bf16[64,512]{1,0:T(8,128)(2,1)S(1)}, bf16[64,512]{1,0:T(8,128)(2,1)S(1)}, u32[]{:S(2)}, u32[]{:S(2)}) collective-permute-start(bf16[64,512]{1,0:T(8,128)(2,1)S(1)} %fusion.49), channel_id=1, source_target_pairs={{0,32},{32,64},{64,96},{96,0},{1,33},{33,65},{65,97},{97,1},{2,34}... | collective-permute-start | bytes 196616 | tf_op jit(solution)/shard_map/ppermute | solution.py:312
  31.3 6.2 %collective-permute-start.3 = (bf16[64,2048]{1,0:T(8,128)(2,1)S(1)}, bf16[64,2048]{1,0:T(8,128)(2,1)S(1)}, u32[]{:S(2)}, u32[]{:S(2)}) collective-permute-start(bf16[64,2048]{1,0:T(8,128)(2,1)S(1)} %collective-permute-done), channel_id=1, source_target_pairs={{0,96},{32,0},{64,32},{96,64},{1,97},{33,1},{65,33},{97,65},{2,98}... | collective-permute-start | bytes 786440 | tf_op jit(solution)/shard_map/ppermute | solution.py:312
  36.1 6.7 %copy-start = (bf16[64,2048]{1,0:T(8,128)(2,1)S(1)}, bf16[64,2048]{1,0:T(8,128)(2,1)}, u32[]{:S(2)}) copy-start(bf16[64,2048]{1,0:T(8,128)(2,1)} %param.19) | copy-start | bytes 786436
  36.1 6.9 %copy-start.3 = (f32[2048]{0:T(1024)S(1)}, f32[2048]{0:T(1024)}, u32[]{:S(2)}) copy-start(f32[2048]{0:T(1024)} %param.30) | copy-start | bytes 24580
  38.0 4.7 %collective-permute-start.6 = (bf16[64,512]{1,0:T(8,128)(2,1)S(1)}, bf16[64,512]{1,0:T(8,128)(2,1)S(1)}, u32[]{:S(2)}, u32[]{:S(2)}) collective-permute-start(bf16[64,512]{1,0:T(8,128)(2,1)S(1)} %fusion.46), channel_id=1, source_target_pairs={{0,64},{32,96},{64,0},{96,32},{1,65},{33,97},{65,1},{97,33},{2,66}... | collective-permute-start | bytes 196616 | tf_op jit(solution)/shard_map/ppermute | solution.py:312
  45.4 45.1 %all-to-all-start.1 = ((bf16[128,8,1024]{2,1,0:T(8,128)(2,1)}), bf16[128,8,1024]{2,1,0:T(8,128)(2,1)S(1)}, u32[]{:S(2)}, u32[]{:S(2)}) async-start(bf16[128,8,1024]{2,1,0:T(8,128)(2,1)} %convert_bitcast_fusion), calls=%async_computation.1 | async-start | bytes 4194304 | tf_op jit(solution)/shard_map/all_to_all | solution.py:393
  90.4 35.7 %all-to-all-start = ((bf16[128,8,1024]{2,1,0:T(8,128)(2,1)}), bf16[128,8,1024]{2,1,0:T(8,128)(2,1)}, u32[]{:S(2)}, u32[]{:S(2)}) async-start(bf16[128,8,1024]{2,1,0:T(8,128)(2,1)} %convert_bitcast_fusion.1), calls=%async_computation | async-start | bytes 4194304 | tf_op jit(solution)/shard_map/all_to_all | solution.py:393
  95.9 5.1 %copy-start.6 = (bf16[1,2048,768]{2,1,0:T(8,128)(2,1)S(1)}, bf16[1,2048,768]{2,1,0:T(8,128)(2,1)}, u32[]{:S(2)}) copy-start(bf16[1,2048,768]{2,1,0:T(8,128)(2,1)} %param.33) | copy-start | bytes 9437188
  179.5 35.0 %all-to-all-start.2 = ((bf16[128,8,1024]{2,1,0:T(8,128)(2,1)}), bf16[128,8,1024]{2,1,0:T(8,128)(2,1)S(1)}, u32[]{:S(2)}, u32[]{:S(2)}) async-start(bf16[128,8,1024]{2,1,0:T(8,128)(2,1)} %bitcast.101), calls=%async_computation.2 | async-start | bytes 4194304 | tf_op jit(solution)/shard_map/all_to_all | solution.py:393
  183.9 4.4 %copy-start.4 = (f32[64,8]{0,1:T(8,128)S(1)}, f32[64,8]{0,1:T(8,128)}, u32[]{:S(2)}) copy-start(f32[64,8]{0,1:T(8,128)} %param.32) | copy-start | bytes 6148
where the time goes:
time: 217 us; the launch traced here: 216 us
  waiting for transfers between devices  81.3 us (37%)
  starting transfers between devices  37 us (17%)
  blocking collectives  35.9 us (17%)
  Pallas kernels  32.8 us (15%)
  matrix products  24.3 us (11%)
  between operations  2.22 us (1%)
    all_to_all x3, waiting for transfers between devices, swap(): lax.all_to_all(x.reshape(expert_count, capacity, -1), ('req', 'exp'), spl...  73.7 us
    all_to_all x1, blocking collectives, swap(): lax.all_to_all(x.reshape(expert_count, capacity, -1), ('req', 'exp'), spl...  35.9 us
    all_to_all x3, starting transfers between devices, swap(): lax.all_to_all(x.reshape(expert_count, capacity, -1), ('req', 'exp'), spl...  24.5 us
    dot_general x15, matrix products, matmul(): return jnp.dot(a, b, preferred_element_type=F32)  24.3 us
    ppermute x9, starting transfers between devices, shift(): return lax.ppermute(x, 'req', [(i, (i + by) % size) for i in range(size)])  12.5 us
    pallas_call x1, Pallas kernels, second_half(): pl.pallas_call(second_kernel, grid=(count // rows,), in_specs=[by_rows(co...  12.1 us
    pallas_call x2, Pallas kernels, attention(): pl.pallas_call(functools.partial(attention_kernel, made is None, span), g...  11 us
    ppermute x9, waiting for transfers between devices, shift(): return lax.ppermute(x, 'req', [(i, (i + by) % size) for i in range(size)])  7.58 us
  transfers between devices with their start and end apart: 12, of which 7 were waited for; matrix products, arithmetic and copies ran while one was open for 10% of the time, Pallas kernels for 4%

commit v1 on v0

--- a/solution.py
+++ b/solution.py
@@ -230,60 +230,113 @@
     )(length, place, cache, *fresh)
 
 
-def second_kernel(x_ref, gate_ref, up_ref, down_ref, gate_in, up_in, hidden_out, sent_out):
-    x = x_ref[...]
-    gate = matmul(x, gate_ref[...]) + gate_in[...]
-    up = matmul(x, up_ref[...]) + up_in[...]
-    hidden = (gate / (1.0 + jnp.exp(-gate)) * up).astype(BF16)
-    hidden_out[...] = hidden
-    sent_out[...] = matmul(hidden, down_ref[...]).astype(BF16)
-
-
-def second_half(x, w_gate, w_up, w_down, gate, up):
-    count, cols = x.shape
-    width = w_gate.shape[1]
-    rows = 128
-    once = pl.Buffered(1)
-    by_rows = lambda n: pl.BlockSpec((rows, n), lambda i: (i, 0))
-    part = pl.BlockSpec((cols, width), lambda i: (1, 0), pipeline_mode=once)
-    down = pl.BlockSpec((width, cols), lambda i: (0, 0), pipeline_mode=once)
-    return pl.pallas_call(
-        second_kernel,
-        grid=(count // rows,),
-        in_specs=[by_rows(cols), part, part, down, by_rows(width), by_rows(width)],
-        out_specs=[by_rows(width), by_rows(cols)],
-        out_shape=[
-            jax.ShapeDtypeStruct((count, width), BF16),
-            jax.ShapeDtypeStruct((count, cols), BF16),
-        ],
-        name="experts_second",
-        cost_estimate=pl.CostEstimate(
-            flops=6 * count * cols * width, bytes_accessed=16 << 20, transcendentals=count * width
-        ),
-    )(x, w_gate, w_up, w_down, gate, up)
-
-
-def down_kernel(hidden_ref, down_ref, out_ref):
-    out_ref[...] = matmul(hidden_ref[...], down_ref[...]).astype(BF16)
-
-
-def last_columns(hidden, w_down, cols):
-    count, width = hidden.shape
+def outbox_kernel(pick_ref, middle_ref, gain_ref, out_ref, normed_ref):
+    @pl.when(pl.program_id(0) == 0)
+    def _():
+        middle = middle_ref[...].astype(F32)
+        power = jnp.mean(middle * middle, axis=-1, keepdims=True)
+        normed_ref[...] = (middle * lax.rsqrt(power + NORM_EPS) * gain_ref[...]).astype(BF16)
+
+    out_ref[...] = matmul(pick_ref[...], normed_ref[...]).astype(BF16)
+
+
+def outbox(pick, middle, gain):
+    count, tokens = pick.shape
+    width = middle.shape[1]
     rows = 256
     return pl.pallas_call(
-        down_kernel,
+        outbox_kernel,
         grid=(count // rows,),
         in_specs=[
-            pl.BlockSpec((rows, width), lambda i: (i, 0)),
-            pl.BlockSpec((width, cols), lambda i: (0, 1), pipeline_mode=pl.Buffered(1)),
+            pl.BlockSpec((rows, tokens), lambda i: (i, 0)),
+            pl.BlockSpec((tokens, width), lambda i: (0, 0)),
+            pl.BlockSpec((1, width), lambda i: (0, 0)),
         ],
-        out_specs=pl.BlockSpec((rows, cols), lambda i: (i, 0)),
-        out_shape=jax.ShapeDtypeStruct((count, cols), BF16),
-        name="experts_third",
+        out_specs=pl.BlockSpec((rows, width), lambda i: (i, 0)),
+        out_shape=jax.ShapeDtypeStruct((count, width), BF16),
+        scratch_shapes=[pltpu.VMEM((tokens, width), BF16)],
+        name="outbox",
         cost_estimate=pl.CostEstimate(
-            flops=2 * count * cols * width, bytes_accessed=5 << 20, transcendentals=0
-        ),
-    )(hidden, w_down)
+            flops=2 * count * tokens * width, bytes_accessed=2 * count * width, transcendentals=0
+        ),
+    )(pick, middle, gain)
+
+
+INNER = 3
+OUTER = 2
+
+
+def experts_kernel(x_ref, gate_ref, up_ref, down_ref, out_ref, hidden_ref):
+    step = pl.program_id(1)
+
+    @pl.when(step < INNER)
+    def _():
+        x = x_ref[...]
+        gate = matmul(x, gate_ref[...])
+        up = matmul(x, up_ref[...])
+        hidden_ref[step] = (gate / (1.0 + jnp.exp(-gate)) * up).astype(BF16)
+
+    @pl.when(step >= INNER)
+    def _():
+        hidden = jnp.concatenate([hidden_ref[j] for j in range(INNER)], axis=1)
+        out_ref[...] = matmul(hidden, down_ref[...]).astype(BF16)
+
+
+def experts(x, w_gate, w_up, w_down):
+    count, width = x.shape
+    inner = w_gate.shape[1]
+    rows = count // 2
+    cut = inner // INNER
+    cols = width // OUTER
+    entry = pl.BlockSpec((width, cut), lambda i, j: (0, jnp.where(j < INNER, j, 0)))
+    leave = lambda j: jnp.maximum(j - INNER, 0)
+    return pl.pallas_call(
+        experts_kernel,
+        grid=(2, INNER + OUTER),
+        in_specs=[
+            pl.BlockSpec((rows, width), lambda i, j: (i, 0)),
+            entry,
+            entry,
+            pl.BlockSpec((inner, cols), lambda i, j: (0, leave(j))),
+        ],
+        out_specs=pl.BlockSpec((rows, cols), lambda i, j: (i, leave(j))),
+        out_shape=jax.ShapeDtypeStruct((count, width), BF16),
+        scratch_shapes=[pltpu.VMEM((INNER, rows, cut), BF16)],
+        name="experts",
+        cost_estimate=pl.CostEstimate(
+            flops=6 * count * width * inner,
+            bytes_accessed=4 * count * width + 12 * width * inner,
+            transcendentals=count * inner,
+        ),
+    )(x, w_gate, w_up, w_down)
+
+
+def combine_kernel(mix_ref, middle_ref, returned_ref, out_ref):
+    mixture = matmul(mix_ref[...], returned_ref[...])
+    tokens = middle_ref.shape[0]
+    mixture = mixture[:tokens] + mixture[tokens:]
+    out_ref[...] = (middle_ref[...].astype(F32) + mixture).astype(BF16)
+
+
+def combine(mix, middle, returned):
+    count, width = returned.shape
+    tokens = middle.shape[0]
+    cols = width // 4
+    return pl.pallas_call(
+        combine_kernel,
+        grid=(4,),
+        in_specs=[
+            pl.BlockSpec(mix.shape, lambda i: (0, 0)),
+            pl.BlockSpec((tokens, cols), lambda i: (0, i)),
+            pl.BlockSpec((count, cols), lambda i: (0, i)),
+        ],
+        out_specs=pl.BlockSpec((tokens, cols), lambda i: (0, i)),
+        out_shape=jax.ShapeDtypeStruct(middle.shape, BF16),
+        name="combine",
+        cost_estimate=pl.CostEstimate(
+            flops=4 * tokens * count * width, bytes_accessed=2 * count * width, transcendentals=0
+        ),
+    )(mix, middle, returned)
 
 
 def slot_table(routes, expert_count, capacity):
@@ -338,7 +391,6 @@
     top_count = routes.shape[1]
     capacity = max(2, 2 * tok_rows * top_count // expert_count)
     slot_count = expert_count * capacity
-    half = model_width // 2
 
     attend = functools.partial(
         attention,
@@ -385,30 +437,19 @@
         columns.append(column)
     projected = jnp.concatenate(columns, axis=1).astype(F32)
     middle = (residual.astype(F32) + projected).astype(BF16)
-    middle32 = middle.astype(F32)
-    power = jnp.mean(middle32 * middle32, axis=-1, keepdims=True)
-    normed = (middle32 * lax.rsqrt(power + NORM_EPS) * post_gain).astype(BF16)
 
     def swap(x):
         return lax.all_to_all(
-            x.reshape(expert_count, capacity, -1),
+            x.reshape(expert_count, capacity, model_width),
             ("req", "exp"),
             split_axis=0,
             concat_axis=0,
             tiled=True,
-        ).reshape(slot_count, -1)
-
-    parts = (slice(0, half), slice(half, model_width))
-    arrived = [swap(matmul(pick, normed[:, part]).astype(BF16)) for part in parts]
-    gate = matmul(arrived[0], w_gate[0, parts[0]])
-    up = matmul(arrived[0], w_up[0, parts[0]])
-    hidden, sent = second_half(arrived[1], w_gate[0], w_up[0], w_down[0], gate, up)
-    sent = [sent, last_columns(hidden, w_down[0], half)]
-    outs = []
-    for part, out in zip(parts, sent):
-        mixture = matmul(mix, swap(out))
-        outs.append(middle32[:, part] + (mixture[:tok_rows] + mixture[tok_rows:]))
-    hidden_out = jnp.concatenate(outs, axis=1).astype(BF16)
+        ).reshape(slot_count, model_width)
+
+    arrived = swap(outbox(pick, middle, post_gain[None]))
+    returned = swap(experts(arrived, w_gate[0], w_up[0], w_down[0]))
+    hidden_out = combine(mix, middle, returned)
     return (hidden_out, new_keys[None], new_values[None])
 
 

time: 217 us -> 198 us (0.912)
  blocking collectives: 35.9 us -> 67.5 us
  waiting for transfers between devices: 81.3 us -> 54 us
  starting transfers between devices: 37 us -> 17.9 us
  matrix products: 24.3 us -> 8.91 us
  Pallas kernels: 32.8 us -> 43.2 us
    all_to_all x1, blocking collectives: 35.9 us -> 67.5 us  [swap(): lax.all_to_all(x.reshape(expert_count, capacity, model_width), ('req', 'e...]
    all_to_all x3 -> x1, waiting for transfers between devices: 73.7 us -> 47.2 us  [swap(): lax.all_to_all(x.reshape(expert_count, capacity, model_width), ('req', 'e...]
    all_to_all x3 -> x1, starting transfers between devices: 24.5 us -> 5.52 us  [swap(): lax.all_to_all(x.reshape(expert_count, capacity, model_width), ('req', 'e...]
    dot_general x15 -> x9, matrix products: 24.3 us -> 8.91 us  [matmul(): return jnp.dot(a, b, preferred_element_type=F32)]
    pallas_call x2 -> x3, Pallas kernels: 17.4 us -> 27.8 us  [the longest x1 18.4 us: experts(): pl.pallas_call(experts_kernel, grid=(2, INNER + OUTER), in_specs=[pl.Bloc...]
  transfers between devices with their start and end apart: 12 -> 10, of which waited for: 7 -> 5; matrix products, arithmetic and copies ran while one was open for 10% -> 6% of each run, Pallas kernels for 4% -> 5%
where the time goes in v1:
time: 198 us; the launch traced here: 197 us
  blocking collectives  67.5 us (34%)
  waiting for transfers between devices  54 us (27%)
  Pallas kernels  43.2 us (22%)
  starting transfers between devices  17.9 us (9%)
  matrix products  8.91 us (4%)
  other arithmetic  3.48 us (2%)
  between operations  2.17 us (1%)
    all_to_all x1, blocking collectives, swap(): lax.all_to_all(x.reshape(expert_count, capacity, model_width), ('req', 'e...  67.5 us
    all_to_all x1, waiting for transfers between devices, swap(): lax.all_to_all(x.reshape(expert_count, capacity, model_width), ('req', 'e...  47.2 us
    pallas_call x1, Pallas kernels, experts(): pl.pallas_call(experts_kernel, grid=(2, INNER + OUTER), in_specs=[pl.Bloc...  18.4 us
    ppermute x9, starting transfers between devices, shift(): return lax.ppermute(x, 'req', [(i, (i + by) % size) for i in range(size)])  12.3 us
    pallas_call x2, Pallas kernels, attention(): pl.pallas_call(functools.partial(attention_kernel, made is None, span), g...  11 us
    dot_general x9, matrix products, matmul(): return jnp.dot(a, b, preferred_element_type=F32)  8.91 us
    ppermute x9, waiting for transfers between devices, shift(): return lax.ppermute(x, 'req', [(i, (i + by) % size) for i in range(size)])  6.83 us
    all_to_all x1, starting transfers between devices, swap(): lax.all_to_all(x.reshape(expert_count, capacity, model_width), ('req', 'e...  5.52 us
  transfers between devices with their start and end apart: 10, of which 5 were waited for; matrix products, arithmetic and copies ran while one was open for 6% of the time, Pallas kernels for 5%

profile of v1, /device:TPU:1, one launch (start us, length us, event | category | flops | bytes accessed | tf_op | source)
XLA Modules:
  0.0 197.4 jit_solution(3035279468119975392)
XLA Ops:
  1.9 0.0 copy-start.1
  1.9 6.1 %shard_map.202 = (bf16[64,2048]{1,0:T(8,128)(2,1)}, bf16[64,256]{1,0:T(8,128)(2,1)}, f32[64,128]{1,0:T(8,128)}, f32[64,128]{1,0:T(8,128)}, f32[64,128]{1,0:T(8,128)}, /*index=5*/bf16[80,64]{1,0:T(8,128)(2,1)}) custom-call(s32[1]{0:T(128)S(6)} %copy.31.refs_0_.length_ref, s32[1]{0:T(128)S(6)} %copy.32.refs_1_, f32[1,128]{1,0:T(1,128)} %bitcast.86, ...), custom_call_target="tpu_custom_call" | custom-call | flops 402653184 | bytes 2097152 | tf_op jit(solution)/shard_map/pallas_call | solution.py:181
  8.0 0.0 copy-start.5
  8.1 3.6 %collective-permute-start = (bf16[64,2048]{1,0:T(8,128)(2,1)}, bf16[64,2048]{1,0:T(8,128)(2,1)S(1)}, u32[]{:S(2)}, u32[]{:S(2)}) collective-permute-start(bf16[64,2048]{1,0:T(8,128)(2,1)} %get-tuple-element.11), channel_id=1, source_target_pairs={{0,96},{32,0},{64,32},{96,64},{1,97},{33,1},{65,33},{97,65},{2,98}... | collective-permute-start | bytes 786440 | tf_op jit(solution)/shard_map/ppermute | solution.py:365
  11.7 0.0 collective-permute-start.7
  11.7 4.9 %shard_map.203 = (bf16[64,2048]{1,0:T(8,128)(2,1)}, bf16[64,256]{1,0:T(8,128)(2,1)}) custom-call(s32[1]{0:T(128)S(6)} %copy.31.refs_0_.length_ref, s32[1]{0:T(128)S(6)} %copy.32.refs_1_, f32[1,128]{1,0:T(1,128)} %bitcast.87, f32[1,128]{1,0:T(1,128)} %bitcast.89, bf16[64,4096]{1,0:T(8,128)(2,1)} %refs_4_.3, bf16[64,1024]{1,0:T(8,128)(2,1)} %rest_0_.1, ...), custom_call_target="tpu_custom_call" | custom-call | flops 402653184 | bytes 2097152 | tf_op jit(solution)/shard_map/pallas_call | solution.py:181
  16.6 0.0 collective-permute-start.4
  16.6 2.7 %collective-permute-start.1 = (bf16[64,2048]{1,0:T(8,128)(2,1)}, bf16[64,2048]{1,0:T(8,128)(2,1)S(1)}, u32[]{:S(2)}, u32[]{:S(2)}) collective-permute-start(bf16[64,2048]{1,0:T(8,128)(2,1)} %get-tuple-element.15), channel_id=1, source_target_pairs={{0,96},{32,0},{64,32},{96,64},{1,97},{33,1},{65,33},{97,65},{2,98}... | collective-permute-start | bytes 786440 | tf_op jit(solution)/shard_map/ppermute | solution.py:365
  19.4 2.2 %fusion = f32[64,512]{1,0:T(8,128)S(1)} fusion(bf16[64,2048]{1,0:T(8,128)(2,1)} %get-tuple-element.15, bf16[4096,512]{1,0:T(8,128)(2,1)} %param.29), kind=kOutput, calls=%fused_computation | convolution fusion | flops 134217728 | bytes 2490368 | tf_op jit(solution)/shard_map/dot_general | solution.py:26
  21.5 0.1 copy.29
  21.6 0.2 fusion.49
  21.8 0.1 fusion.50
  21.9 0.2 select_reduce_fusion
  22.2 0.1 copy.30
  22.2 2.2 %fusion.28 = bf16[64,512]{1,0:T(8,128)(2,1)S(1)} fusion(f32[64,512]{1,0:T(8,128)S(1)} %fusion, bf16[64,2048]{1,0:T(8,128)(2,1)S(1)} %copy-done.5, bf16[4096,512]{1,0:T(8,128)(2,1)} %param.29), kind=kOutput, calls=%fused_computation.20 | convolution fusion | flops 134283264 | bytes 2555904 | tf_op jit(solution)/shard_map/dot_general | solution.py:26
  24.5 1.8 collective-permute-done.4
  26.3 2.1 %fusion.2 = f32[64,512]{1,0:T(8,128)S(1)} fusion(bf16[64,2048]{1,0:T(8,128)(2,1)S(1)} %collective-permute-done.4, bf16[4096,512]{1,0:T(8,128)(2,1)} %param.29), kind=kOutput, calls=%fused_computation.2 | convolution fusion | flops 134217728 | bytes 2490368 | tf_op jit(solution)/shard_map/dot_general | solution.py:26
  28.4 0.0 collective-permute-done.7
  28.4 0.5 fusion.31
  28.9 0.1 collective-permute-start.8
  29.0 1.5 collective-permute-start.5
  30.4 0.0 collective-permute-done.1
  30.4 0.5 fusion.6
  30.9 0.0 copy-start
  30.9 0.5 fusion.37
  31.4 0.1 collective-permute-start.2
  31.5 2.7 %collective-permute-start.3 = (bf16[64,2048]{1,0:T(8,128)(2,1)S(1)}, bf16[64,2048]{1,0:T(8,128)(2,1)S(1)}, u32[]{:S(2)}, u32[]{:S(2)}) collective-permute-start(bf16[64,2048]{1,0:T(8,128)(2,1)S(1)} %collective-permute-done), channel_id=1, source_target_pairs={{0,96},{32,0},{64,32},{96,64},{1,97},{33,1},{65,33},{97,65},{2,98}... | collective-permute-start | bytes 786440 | tf_op jit(solution)/shard_map/ppermute | solution.py:365
  34.1 1.8 collective-permute-done.5
  36.0 0.5 fusion.4
  36.5 1.4 collective-permute-done.3
  37.8 0.5 fusion.34
  38.3 1.7 collective-permute-start.6
  40.0 1.2 fusion.47.pick_ref
  41.2 0.0 collective-permute-done.8
  41.2 0.0 collective-permute-done.2
  41.2 1.8 collective-permute-done.6
  43.0 0.8 add_convert_fusion.middle_ref
  43.8 4.8 %outbox.1 = bf16[1024,2048]{1,0:T(8,128)(2,1)} custom-call(bf16[1024,64]{1,0:T(8,128)(2,1)} %fusion.47.pick_ref, bf16[64,2048]{1,0:T(8,128)(2,1)} %add_convert_fusion.middle_ref, f32[1,2048]{1,0:T(1,128)} %bitcast.85), custom_call_target="tpu_custom_call" | custom-call | flops 268435456 | bytes 4194304 | tf_op jit(solution)/shard_map/outbox/pallas_call | solution.py:247
  48.6 67.5 %all_to_all.10 = bf16[128,8,2048]{2,1,0:T(8,128)(2,1)} all-to-all(bf16[128,8,2048]{2,1,0:T(8,128)(2,1)} %bitcast.73), channel_id=1, replica_groups=mesh['req'=4,'exp'=32] {'req','exp'}, dimensions={0} | all-to-all | bytes 8388608 | tf_op jit(solution)/shard_map/all_to_all | solution.py:442
  116.2 18.4 %experts.1 = bf16[1024,2048]{1,0:T(8,128)(2,1)} custom-call(bf16[1024,2048]{1,0:T(8,128)(2,1)} %bitcast.81, bf16[2048,768]{1,0:T(8,128)(2,1)} %bitcast.90, bf16[2048,768]{1,0:T(8,128)(2,1)} %bitcast.91, bf16[768,2048]{1,0:T(8,128)(2,1)} %bitcast.92), custom_call_target="tpu_custom_call" | custom-call | flops 9663676416 | bytes 27262976 | tf_op jit(solution)/shard_map/experts/pallas_call | solution.py:293
  134.6 5.5 %all-to-all-start.1 = ((bf16[128,8,2048]{2,1,0:T(8,128)(2,1)}), bf16[128,8,2048]{2,1,0:T(8,128)(2,1)}, u32[]{:S(2)}, u32[]{:S(2)}) async-start(bf16[128,8,2048]{2,1,0:T(8,128)(2,1)} %bitcast.80), calls=%async_computation.1 | async-start | bytes 8388608 | tf_op jit(solution)/shard_map/all_to_all | solution.py:442
  140.1 0.0 copy-start.3
  140.2 2.2 %shard_map.205 = bf16[1024,512]{1,0:T(8,128)(2,1)} custom-call(s32[1]{0:T(128)S(6)} %copy.31.refs_0_.length_ref, bf16[80,64]{1,0:T(8,128)(2,1)} %get-tuple-element.16.place_ref, bf16[1024,512]{1,0:T(8,128)(2,1)} %bitcast.76, bf16[64,1024]{1,0:T(8,128)(2,1)} %rest_0_.1), custom_call_target="tpu_custom_call" | custom-call | flops 5242880 | bytes 2097152 | tf_op jit(solution)/shard_map/pallas_call | solution.py:218
  142.3 2.2 %shard_map.204 = bf16[1024,512]{1,0:T(8,128)(2,1)} custom-call(s32[1]{0:T(128)S(6)} %copy.31.refs_0_.length_ref, bf16[80,64]{1,0:T(8,128)(2,1)} %get-tuple-element.16.place_ref, bf16[1024,512]{1,0:T(8,128)(2,1)} %bitcast.79, bf16[64,256]{1,0:T(8,128)(2,1)} %get-tuple-element.17.rest_0_, bf16[64,256]{1,0:T(8,128)(2,1)} %get-tuple-element.18.rest_1_), custom_call_target="tpu_custom_call" | custom-call | flops 5242880 | bytes 2097152 | tf_op jit(solution)/shard_map/pallas_call | solution.py:218
  144.6 0.4 reduce-precision_convert_fusion
  144.9 0.7 pad_maximum_fusion.mix_ref
  145.7 47.2 %all-to-all-done.1 = bf16[128,8,2048]{2,1,0:T(8,128)(2,1)} async-done(((bf16[128,8,2048]{2,1,0:T(8,128)(2,1)}), bf16[128,8,2048]{2,1,0:T(8,128)(2,1)}, u32[]{:S(2)}, u32[]{:S(2)}) %all-to-all-start.1) | async-done | bytes 4194336 | tf_op jit(solution)/shard_map/all_to_all | solution.py:442
  192.9 4.5 %combine.1 = bf16[64,2048]{1,0:T(8,128)(2,1)} custom-call(bf16[128,1024]{1,0:T(8,128)(2,1)} %pad_maximum_fusion.mix_ref, bf16[64,2048]{1,0:T(8,128)(2,1)} %add_convert_fusion.middle_ref, bf16[1024,2048]{1,0:T(8,128)(2,1)} %bitcast.36.returned_ref), custom_call_target="tpu_custom_call" | custom-call | flops 536870912 | bytes 4194304 | tf_op jit(solution)/shard_map/combine/pallas_call | solution.py:325
  (14 shorter events, 0.1 us)
Async XLA Ops:
  1.9 19.6 %copy-start.2 = (s32[64,8]{0,1:T(8,128)S(1)}, s32[64,8]{0,1:T(8,128)}, u32[]{:S(2)}) copy-start(s32[64,8]{0,1:T(8,128)} %param.31) | copy-start | bytes 6148
  1.9 19.9 %copy-start.1 = (bf16[64,64]{1,0:T(8,128)(2,1)S(1)}, bf16[64,64]{1,0:T(8,128)(2,1)}, u32[]{:S(2)}) copy-start(bf16[64,64]{1,0:T(8,128)(2,1)} %constant.41.clone) | copy-start | bytes 24580
  8.0 14.2 %copy-start.5 = (bf16[64,2048]{1,0:T(8,128)(2,1)S(1)}, bf16[64,2048]{1,0:T(8,128)(2,1)}, u32[]{:S(2)}) copy-start(bf16[64,2048]{1,0:T(8,128)(2,1)} %get-tuple-element.11) | copy-start | bytes 786436
  8.1 22.8 %collective-permute-start = (bf16[64,2048]{1,0:T(8,128)(2,1)}, bf16[64,2048]{1,0:T(8,128)(2,1)S(1)}, u32[]{:S(2)}, u32[]{:S(2)}) collective-permute-start(bf16[64,2048]{1,0:T(8,128)(2,1)} %get-tuple-element.11), channel_id=1, source_target_pairs={{0,96},{32,0},{64,32},{96,64},{1,97},{33,1},{65,33},{97,65},{2,98}... | collective-permute-start | bytes 786440 | tf_op jit(solution)/shard_map/ppermute | solution.py:365
  11.7 16.7 %collective-permute-start.7 = (bf16[64,2048]{1,0:T(8,128)(2,1)}, bf16[64,2048]{1,0:T(8,128)(2,1)S(1)}, u32[]{:S(2)}, u32[]{:S(2)}) collective-permute-start(bf16[64,2048]{1,0:T(8,128)(2,1)} %get-tuple-element.11), channel_id=1, source_target_pairs={{0,32},{32,64},{64,96},{96,0},{1,33},{33,65},{65,97},{97,1},{2,34}... | collective-permute-start | bytes 786440 | tf_op jit(solution)/shard_map/ppermute | solution.py:365
  16.6 9.7 %collective-permute-start.4 = (bf16[64,2048]{1,0:T(8,128)(2,1)}, bf16[64,2048]{1,0:T(8,128)(2,1)S(1)}, u32[]{:S(2)}, u32[]{:S(2)}) collective-permute-start(bf16[64,2048]{1,0:T(8,128)(2,1)} %get-tuple-element.15), channel_id=1, source_target_pairs={{0,32},{32,64},{64,96},{96,0},{1,33},{33,65},{65,97},{97,1},{2,34}... | collective-permute-start | bytes 786440 | tf_op jit(solution)/shard_map/ppermute | solution.py:365
  16.6 13.8 %collective-permute-start.1 = (bf16[64,2048]{1,0:T(8,128)(2,1)}, bf16[64,2048]{1,0:T(8,128)(2,1)S(1)}, u32[]{:S(2)}, u32[]{:S(2)}) collective-permute-start(bf16[64,2048]{1,0:T(8,128)(2,1)} %get-tuple-element.15), channel_id=1, source_target_pairs={{0,96},{32,0},{64,32},{96,64},{1,97},{33,1},{65,33},{97,65},{2,98}... | collective-permute-start | bytes 786440 | tf_op jit(solution)/shard_map/ppermute | solution.py:365
  22.2 6.2 %copy-start.4 = (bf16[4096,512]{1,0:T(8,128)(2,1)S(1)}, bf16[4096,512]{1,0:T(8,128)(2,1)}, u32[]{:S(2)}) copy-start(bf16[4096,512]{1,0:T(8,128)(2,1)} %param.29) | copy-start | bytes 12582916
  28.9 12.3 %collective-permute-start.8 = (bf16[64,512]{1,0:T(8,128)(2,1)S(1)}, bf16[64,512]{1,0:T(8,128)(2,1)S(1)}, u32[]{:S(2)}, u32[]{:S(2)}) collective-permute-start(bf16[64,512]{1,0:T(8,128)(2,1)S(1)} %fusion.31), channel_id=1, source_target_pairs={{0,96},{32,0},{64,32},{96,64},{1,97},{33,1},{65,33},{97,65},{2,98}... | collective-permute-start | bytes 196616 | tf_op jit(solution)/shard_map/ppermute | solution.py:365
  29.0 7.0 %collective-permute-start.5 = (bf16[64,2048]{1,0:T(8,128)(2,1)S(1)}, bf16[64,2048]{1,0:T(8,128)(2,1)S(1)}, u32[]{:S(2)}, u32[]{:S(2)}) collective-permute-start(bf16[64,2048]{1,0:T(8,128)(2,1)S(1)} %collective-permute-done.4), channel_id=1, source_target_pairs={{0,32},{32,64},{64,96},{96,0},{1,33},{33,65},{65,97},{97,1},{2,34}... | collective-permute-start | bytes 786440 | tf_op jit(solution)/shard_map/ppermute | solution.py:365
  30.9 12.2 %copy-start = (bf16[64,2048]{1,0:T(8,128)(2,1)S(1)}, bf16[64,2048]{1,0:T(8,128)(2,1)}, u32[]{:S(2)}) copy-start(bf16[64,2048]{1,0:T(8,128)(2,1)} %param.19) | copy-start | bytes 786436
  31.4 9.8 %collective-permute-start.2 = (bf16[64,512]{1,0:T(8,128)(2,1)S(1)}, bf16[64,512]{1,0:T(8,128)(2,1)S(1)}, u32[]{:S(2)}, u32[]{:S(2)}) collective-permute-start(bf16[64,512]{1,0:T(8,128)(2,1)S(1)} %fusion.37), channel_id=1, source_target_pairs={{0,32},{32,64},{64,96},{96,0},{1,33},{33,65},{65,97},{97,1},{2,34}... | collective-permute-start | bytes 196616 | tf_op jit(solution)/shard_map/ppermute | solution.py:365
  31.5 6.3 %collective-permute-start.3 = (bf16[64,2048]{1,0:T(8,128)(2,1)S(1)}, bf16[64,2048]{1,0:T(8,128)(2,1)S(1)}, u32[]{:S(2)}, u32[]{:S(2)}) collective-permute-start(bf16[64,2048]{1,0:T(8,128)(2,1)S(1)} %collective-permute-done), channel_id=1, source_target_pairs={{0,96},{32,0},{64,32},{96,64},{1,97},{33,1},{65,33},{97,65},{2,98}... | collective-permute-start | bytes 786440 | tf_op jit(solution)/shard_map/ppermute | solution.py:365
  38.3 4.7 %collective-permute-start.6 = (bf16[64,512]{1,0:T(8,128)(2,1)S(1)}, bf16[64,512]{1,0:T(8,128)(2,1)S(1)}, u32[]{:S(2)}, u32[]{:S(2)}) collective-permute-start(bf16[64,512]{1,0:T(8,128)(2,1)S(1)} %fusion.34), channel_id=1, source_target_pairs={{0,64},{32,96},{64,0},{96,32},{1,65},{33,97},{65,1},{97,33},{2,66}... | collective-permute-start | bytes 196616 | tf_op jit(solution)/shard_map/ppermute | solution.py:365
  134.6 58.2 %all-to-all-start.1 = ((bf16[128,8,2048]{2,1,0:T(8,128)(2,1)}), bf16[128,8,2048]{2,1,0:T(8,128)(2,1)}, u32[]{:S(2)}, u32[]{:S(2)}) async-start(bf16[128,8,2048]{2,1,0:T(8,128)(2,1)} %bitcast.80), calls=%async_computation.1 | async-start | bytes 8388608 | tf_op jit(solution)/shard_map/all_to_all | solution.py:442
  140.1 4.4 %copy-start.3 = (f32[64,8]{0,1:T(8,128)S(1)}, f32[64,8]{0,1:T(8,128)}, u32[]{:S(2)}) copy-start(f32[64,8]{0,1:T(8,128)} %param.32) | copy-start | bytes 6148

commit v2 on v1

--- a/solution.py
+++ b/solution.py
@@ -230,83 +230,103 @@
     )(length, place, cache, *fresh)
 
 
-def outbox_kernel(pick_ref, middle_ref, gain_ref, out_ref, normed_ref):
-    @pl.when(pl.program_id(0) == 0)
-    def _():
-        middle = middle_ref[...].astype(F32)
-        power = jnp.mean(middle * middle, axis=-1, keepdims=True)
-        normed_ref[...] = (middle * lax.rsqrt(power + NORM_EPS) * gain_ref[...]).astype(BF16)
-
-    out_ref[...] = matmul(pick_ref[...], normed_ref[...]).astype(BF16)
+def blocks(total, count):
+    return [pl.ds(i * (total // count), total // count) for i in range(count)]
+
+
+def outbox_kernel(count, pick_ref, middle_ref, gain_ref, out_hbm, normed_ref, out_buf, sems):
+    middle = middle_ref[...].astype(F32)
+    power = jnp.mean(middle * middle, axis=-1, keepdims=True)
+    normed_ref[...] = (middle * lax.rsqrt(power + NORM_EPS) * gain_ref[...]).astype(BF16)
+    copies = []
+    for i, rows in enumerate(blocks(out_buf.shape[0], count)):
+        out_buf[rows, :] = matmul(pick_ref[rows, :], normed_ref[...]).astype(BF16)
+        copy = pltpu.make_async_copy(out_buf.at[rows], out_hbm.at[rows], sems.at[i])
+        copy.start()
+        copies.append(copy)
+    for copy in copies:
+        copy.wait()
 
 
 def outbox(pick, middle, gain):
-    count, tokens = pick.shape
+    slots, tokens = pick.shape
     width = middle.shape[1]
-    rows = 256
+    count = 4
     return pl.pallas_call(
-        outbox_kernel,
-        grid=(count // rows,),
-        in_specs=[
-            pl.BlockSpec((rows, tokens), lambda i: (i, 0)),
-            pl.BlockSpec((tokens, width), lambda i: (0, 0)),
-            pl.BlockSpec((1, width), lambda i: (0, 0)),
+        functools.partial(outbox_kernel, count),
+        in_specs=[pl.BlockSpec(memory_space=pltpu.VMEM)] * 3,
+        out_specs=pl.BlockSpec(memory_space=pltpu.HBM),
+        out_shape=jax.ShapeDtypeStruct((slots, width), BF16),
+        scratch_shapes=[
+            pltpu.VMEM((tokens, width), BF16),
+            pltpu.VMEM((slots, width), BF16),
+            pltpu.SemaphoreType.DMA((count,)),
         ],
-        out_specs=pl.BlockSpec((rows, width), lambda i: (i, 0)),
-        out_shape=jax.ShapeDtypeStruct((count, width), BF16),
-        scratch_shapes=[pltpu.VMEM((tokens, width), BF16)],
         name="outbox",
         cost_estimate=pl.CostEstimate(
-            flops=2 * count * tokens * width, bytes_accessed=2 * count * width, transcendentals=0
+            flops=2 * slots * tokens * width, bytes_accessed=2 * slots * width, transcendentals=0
         ),
     )(pick, middle, gain)
 
 
-INNER = 3
-OUTER = 2
-
-
-def experts_kernel(x_ref, gate_ref, up_ref, down_ref, out_ref, hidden_ref):
-    step = pl.program_id(1)
-
-    @pl.when(step < INNER)
-    def _():
-        x = x_ref[...]
-        gate = matmul(x, gate_ref[...])
-        up = matmul(x, up_ref[...])
-        hidden_ref[step] = (gate / (1.0 + jnp.exp(-gate)) * up).astype(BF16)
-
-    @pl.when(step >= INNER)
-    def _():
-        hidden = jnp.concatenate([hidden_ref[j] for j in range(INNER)], axis=1)
-        out_ref[...] = matmul(hidden, down_ref[...]).astype(BF16)
+def experts_kernel(
+    count, x_hbm, gate_hbm, up_hbm, down_hbm, out_hbm, x_buf, gate_buf, up_buf, down_buf, out_buf,
+    x_sems, weight_sems, out_sems
+):
+    rows = blocks(x_buf.shape[0], count)
+    low, high = blocks(gate_buf.shape[0], 2)
+    depth = gate_buf.shape[0] // 2
+    copy = pltpu.make_async_copy
+    x_in = [copy(x_hbm.at[r], x_buf.at[r], x_sems.at[i]) for i, r in enumerate(rows)]
+    weights_in = [
+        copy(gate_hbm.at[low], gate_buf.at[low], weight_sems.at[0]),
+        copy(gate_hbm.at[high], gate_buf.at[high], weight_sems.at[1]),
+        copy(up_hbm, up_buf, weight_sems.at[2]),
+        copy(down_hbm, down_buf, weight_sems.at[3]),
+    ]
+    for each in [x_in[0], *weights_in[:3], *x_in[1:], weights_in[3]]:
+        each.start()
+    sent = []
+    for i, r in enumerate(rows):
+        x_in[i].wait()
+        x = x_buf[r, :]
+        if i == 0:
+            weights_in[0].wait()
+            gate = matmul(x[:, :depth], gate_buf[low, :])
+            weights_in[1].wait()
+            gate = gate + matmul(x[:, depth:], gate_buf[high, :])
+            weights_in[2].wait()
+        else:
+            gate = matmul(x, gate_buf[...])
+        up = matmul(x, up_buf[...])
+        hidden = (gate / (1.0 + jnp.exp(-gate)) * up).astype(BF16)
+        if i == 0:
+            weights_in[3].wait()
+        out_buf[r, :] = matmul(hidden, down_buf[...]).astype(BF16)
+        out = copy(out_buf.at[r], out_hbm.at[r], out_sems.at[i])
+        out.start()
+        sent.append(out)
+    for out in sent:
+        out.wait()
 
 
 def experts(x, w_gate, w_up, w_down):
-    count, width = x.shape
+    slots, width = x.shape
     inner = w_gate.shape[1]
-    rows = count // 2
-    cut = inner // INNER
-    cols = width // OUTER
-    entry = pl.BlockSpec((width, cut), lambda i, j: (0, jnp.where(j < INNER, j, 0)))
-    leave = lambda j: jnp.maximum(j - INNER, 0)
+    count = 4
     return pl.pallas_call(
-        experts_kernel,
-        grid=(2, INNER + OUTER),
-        in_specs=[
-            pl.BlockSpec((rows, width), lambda i, j: (i, 0)),
-            entry,
-            entry,
-            pl.BlockSpec((inner, cols), lambda i, j: (0, leave(j))),
-        ],
-        out_specs=pl.BlockSpec((rows, cols), lambda i, j: (i, leave(j))),
-        out_shape=jax.ShapeDtypeStruct((count, width), BF16),
-        scratch_shapes=[pltpu.VMEM((INNER, rows, cut), BF16)],
+        functools.partial(experts_kernel, count),
+        in_specs=[pl.BlockSpec(memory_space=pltpu.HBM)] * 4,
+        out_specs=pl.BlockSpec(memory_space=pltpu.HBM),
+        out_shape=jax.ShapeDtypeStruct(x.shape, BF16),
+        scratch_shapes=[pltpu.VMEM(a.shape, BF16) for a in (x, w_gate, w_up, w_down, x)]
+        + [pltpu.SemaphoreType.DMA((n,)) for n in (count, 4, count)],
+        compiler_params=pltpu.CompilerParams(vmem_limit_bytes=48 << 20),
         name="experts",
         cost_estimate=pl.CostEstimate(
-            flops=6 * count * width * inner,
-            bytes_accessed=4 * count * width + 12 * width * inner,
-            transcendentals=count * inner,
+            flops=6 * slots * width * inner,
+            bytes_accessed=4 * slots * width + 6 * width * inner,
+            transcendentals=slots * inner,
         ),
     )(x, w_gate, w_up, w_down)
 
@@ -321,10 +341,10 @@
 def combine(mix, middle, returned):
     count, width = returned.shape
     tokens = middle.shape[0]
-    cols = width // 4
+    cols = width // 2
     return pl.pallas_call(
         combine_kernel,
-        grid=(4,),
+        grid=(2,),
         in_specs=[
             pl.BlockSpec(mix.shape, lambda i: (0, 0)),
             pl.BlockSpec((tokens, cols), lambda i: (0, i)),

time: 198 us -> 191 us (0.965)
  Pallas kernels: 43.2 us -> 36.6 us
    pallas_call x3, Pallas kernels: 27.8 us -> 21.2 us  [the longest x1 14.1 us: experts(): pl.pallas_call(functools.partial(experts_kernel, count), in_specs=[pl.Blo...]
where the time goes in v2:
time: 191 us
  blocking collectives  67.5 us (35%)
  waiting for transfers between devices  54.1 us (28%)
  Pallas kernels  36.6 us (19%)
  starting transfers between devices  17.9 us (9%)
  matrix products  8.92 us (5%)
  other arithmetic  3.48 us (2%)
  between operations  2.2 us (1%)
    all_to_all x1, blocking collectives, swap(): lax.all_to_all(x.reshape(expert_count, capacity, model_width), ('req', 'e...  67.5 us
    all_to_all x1, waiting for transfers between devices, swap(): lax.all_to_all(x.reshape(expert_count, capacity, model_width), ('req', 'e...  47.2 us
    pallas_call x1, Pallas kernels, experts(): pl.pallas_call(functools.partial(experts_kernel, count), in_specs=[pl.Blo...  14.1 us
    ppermute x9, starting transfers between devices, shift(): return lax.ppermute(x, 'req', [(i, (i + by) % size) for i in range(size)])  12.3 us
    pallas_call x2, Pallas kernels, attention(): pl.pallas_call(functools.partial(attention_kernel, made is None, span), g...  11 us
    dot_general x9, matrix products, matmul(): return jnp.dot(a, b, preferred_element_type=F32)  8.92 us
    ppermute x9, waiting for transfers between devices, shift(): return lax.ppermute(x, 'req', [(i, (i + by) % size) for i in range(size)])  6.86 us
    all_to_all x1, starting transfers between devices, swap(): lax.all_to_all(x.reshape(expert_count, capacity, model_width), ('req', 'e...  5.54 us
  transfers between devices with their start and end apart: 10, of which 5 were waited for; matrix products, arithmetic and copies ran while one was open for 6% of the time, Pallas kernels for 5%

profile of v2, /device:TPU:1, one launch (start us, length us, event | category | flops | bytes accessed | tf_op | source)
XLA Modules:
  0.0 190.9 jit_solution(6321449369756789096)
XLA Ops:
  1.9 0.0 copy-start.2
  1.9 6.1 %shard_map.202 = (bf16[64,2048]{1,0:T(8,128)(2,1)}, bf16[64,256]{1,0:T(8,128)(2,1)}, f32[64,128]{1,0:T(8,128)}, f32[64,128]{1,0:T(8,128)}, f32[64,128]{1,0:T(8,128)}, /*index=5*/bf16[80,64]{1,0:T(8,128)(2,1)}) custom-call(s32[1]{0:T(128)S(6)} %copy.31.refs_0_.length_ref, s32[1]{0:T(128)S(6)} %copy.32.refs_1_, f32[1,128]{1,0:T(1,128)} %bitcast.87, ...), custom_call_target="tpu_custom_call" | custom-call | flops 402653184 | bytes 2097152 | tf_op jit(solution)/shard_map/pallas_call | solution.py:181
  8.0 0.0 copy-start.6
  8.1 3.6 %collective-permute-start = (bf16[64,2048]{1,0:T(8,128)(2,1)}, bf16[64,2048]{1,0:T(8,128)(2,1)S(1)}, u32[]{:S(2)}, u32[]{:S(2)}) collective-permute-start(bf16[64,2048]{1,0:T(8,128)(2,1)} %get-tuple-element.11), channel_id=1, source_target_pairs={{0,96},{32,0},{64,32},{96,64},{1,97},{33,1},{65,33},{97,65},{2,98}... | collective-permute-start | bytes 786440 | tf_op jit(solution)/shard_map/ppermute | solution.py:385
  11.7 0.0 collective-permute-start.7
  11.7 4.9 %shard_map.203 = (bf16[64,2048]{1,0:T(8,128)(2,1)}, bf16[64,256]{1,0:T(8,128)(2,1)}) custom-call(s32[1]{0:T(128)S(6)} %copy.31.refs_0_.length_ref, s32[1]{0:T(128)S(6)} %copy.32.refs_1_, f32[1,128]{1,0:T(1,128)} %bitcast.88, f32[1,128]{1,0:T(1,128)} %bitcast.90, bf16[64,4096]{1,0:T(8,128)(2,1)} %refs_4_.3, bf16[64,1024]{1,0:T(8,128)(2,1)} %rest_0_.1, ...), custom_call_target="tpu_custom_call" | custom-call | flops 402653184 | bytes 2097152 | tf_op jit(solution)/shard_map/pallas_call | solution.py:181
  16.6 0.0 collective-permute-start.4
  16.6 2.7 %collective-permute-start.1 = (bf16[64,2048]{1,0:T(8,128)(2,1)}, bf16[64,2048]{1,0:T(8,128)(2,1)S(1)}, u32[]{:S(2)}, u32[]{:S(2)}) collective-permute-start(bf16[64,2048]{1,0:T(8,128)(2,1)} %get-tuple-element.15), channel_id=1, source_target_pairs={{0,96},{32,0},{64,32},{96,64},{1,97},{33,1},{65,33},{97,65},{2,98}... | collective-permute-start | bytes 786440 | tf_op jit(solution)/shard_map/ppermute | solution.py:385
  19.4 2.2 %fusion = f32[64,512]{1,0:T(8,128)S(1)} fusion(bf16[64,2048]{1,0:T(8,128)(2,1)} %get-tuple-element.15, bf16[4096,512]{1,0:T(8,128)(2,1)} %param.29), kind=kOutput, calls=%fused_computation | convolution fusion | flops 134217728 | bytes 2490368 | tf_op jit(solution)/shard_map/dot_general | solution.py:26
  21.5 0.1 copy.29
  21.6 0.2 fusion.49
  21.8 0.1 fusion.50
  21.9 0.2 select_reduce_fusion
  22.2 0.1 copy.30
  22.3 2.2 %fusion.28 = bf16[64,512]{1,0:T(8,128)(2,1)S(1)} fusion(f32[64,512]{1,0:T(8,128)S(1)} %fusion, bf16[64,2048]{1,0:T(8,128)(2,1)S(1)} %copy-done.6, bf16[4096,512]{1,0:T(8,128)(2,1)} %param.29), kind=kOutput, calls=%fused_computation.20 | convolution fusion | flops 134283264 | bytes 2555904 | tf_op jit(solution)/shard_map/dot_general | solution.py:26
  24.5 1.8 collective-permute-done.4
  26.3 2.1 %fusion.2 = f32[64,512]{1,0:T(8,128)S(1)} fusion(bf16[64,2048]{1,0:T(8,128)(2,1)S(1)} %collective-permute-done.4, bf16[4096,512]{1,0:T(8,128)(2,1)} %param.29), kind=kOutput, calls=%fused_computation.2 | convolution fusion | flops 134217728 | bytes 2490368 | tf_op jit(solution)/shard_map/dot_general | solution.py:26
  28.4 0.0 collective-permute-done.7
  28.4 0.5 fusion.31
  28.9 0.1 collective-permute-start.8
  29.0 1.5 collective-permute-start.5
  30.4 0.0 collective-permute-done.1
  30.4 0.5 fusion.6
  30.9 0.0 copy-start.1
  30.9 0.0 collective-permute-done
  30.9 0.5 fusion.37
  31.4 0.1 collective-permute-start.2
  31.5 2.7 %collective-permute-start.3 = (bf16[64,2048]{1,0:T(8,128)(2,1)S(1)}, bf16[64,2048]{1,0:T(8,128)(2,1)S(1)}, u32[]{:S(2)}, u32[]{:S(2)}) collective-permute-start(bf16[64,2048]{1,0:T(8,128)(2,1)S(1)} %collective-permute-done), channel_id=1, source_target_pairs={{0,96},{32,0},{64,32},{96,64},{1,97},{33,1},{65,33},{97,65},{2,98}... | collective-permute-start | bytes 786440 | tf_op jit(solution)/shard_map/ppermute | solution.py:385
  34.1 1.9 collective-permute-done.5
  36.0 0.5 fusion.4
  36.5 1.4 collective-permute-done.3
  37.8 0.5 fusion.34
  38.3 1.7 collective-permute-start.6
  40.0 1.2 fusion.47.pick_ref
  41.2 1.8 collective-permute-done.6
  43.1 0.8 add_convert_fusion.middle_ref
  43.8 3.6 %outbox.1 = bf16[1024,2048]{1,0:T(8,128)(2,1)} custom-call(bf16[1024,64]{1,0:T(8,128)(2,1)} %fusion.47.pick_ref, bf16[64,2048]{1,0:T(8,128)(2,1)} %add_convert_fusion.middle_ref, f32[1,2048]{1,0:T(1,128)} %bitcast.86), custom_call_target="tpu_custom_call" | custom-call | flops 268435456 | bytes 4194304 | tf_op jit(solution)/shard_map/outbox/pallas_call | solution.py:255
  47.4 0.0 copy-start
  47.5 67.5 %all_to_all.10 = bf16[128,8,2048]{2,1,0:T(8,128)(2,1)} all-to-all(bf16[128,8,2048]{2,1,0:T(8,128)(2,1)} %bitcast.74), channel_id=1, replica_groups=mesh['req'=4,'exp'=32] {'req','exp'}, dimensions={0} | all-to-all | bytes 8388608 | tf_op jit(solution)/shard_map/all_to_all | solution.py:462
  115.0 14.1 %experts.1 = bf16[1024,2048]{1,0:T(8,128)(2,1)} custom-call(bf16[1024,2048]{1,0:T(8,128)(2,1)} %bitcast.82, bf16[2048,768]{1,0:T(8,128)(2,1)S(1)} %bitcast.73, bf16[2048,768]{1,0:T(8,128)(2,1)} %bitcast.91, bf16[768,2048]{1,0:T(8,128)(2,1)} %bitcast.92), custom_call_target="tpu_custom_call" | custom-call | flops 9663676416 | bytes 17825792 | tf_op jit(solution)/shard_map/experts/pallas_call | solution.py:317
  129.1 5.5 %all-to-all-start.1 = ((bf16[128,8,2048]{2,1,0:T(8,128)(2,1)}), bf16[128,8,2048]{2,1,0:T(8,128)(2,1)}, u32[]{:S(2)}, u32[]{:S(2)}) async-start(bf16[128,8,2048]{2,1,0:T(8,128)(2,1)} %bitcast.81), calls=%async_computation.1 | async-start | bytes 8388608 | tf_op jit(solution)/shard_map/all_to_all | solution.py:462
  134.6 0.0 copy-start.4
  134.6 2.2 %shard_map.205 = bf16[1024,512]{1,0:T(8,128)(2,1)} custom-call(s32[1]{0:T(128)S(6)} %copy.31.refs_0_.length_ref, bf16[80,64]{1,0:T(8,128)(2,1)} %get-tuple-element.16.place_ref, bf16[1024,512]{1,0:T(8,128)(2,1)} %bitcast.77, bf16[64,1024]{1,0:T(8,128)(2,1)} %rest_0_.1), custom_call_target="tpu_custom_call" | custom-call | flops 5242880 | bytes 2097152 | tf_op jit(solution)/shard_map/pallas_call | solution.py:218
  136.8 2.2 %shard_map.204 = bf16[1024,512]{1,0:T(8,128)(2,1)} custom-call(s32[1]{0:T(128)S(6)} %copy.31.refs_0_.length_ref, bf16[80,64]{1,0:T(8,128)(2,1)} %get-tuple-element.16.place_ref, bf16[1024,512]{1,0:T(8,128)(2,1)} %bitcast.80, bf16[64,256]{1,0:T(8,128)(2,1)} %get-tuple-element.17.rest_0_, bf16[64,256]{1,0:T(8,128)(2,1)} %get-tuple-element.18.rest_1_), custom_call_target="tpu_custom_call" | custom-call | flops 5242880 | bytes 2097152 | tf_op jit(solution)/shard_map/pallas_call | solution.py:218
  139.0 0.4 reduce-precision_convert_fusion
  139.4 0.7 pad_maximum_fusion.mix_ref
  140.1 47.2 %all-to-all-done.1 = bf16[128,8,2048]{2,1,0:T(8,128)(2,1)} async-done(((bf16[128,8,2048]{2,1,0:T(8,128)(2,1)}), bf16[128,8,2048]{2,1,0:T(8,128)(2,1)}, u32[]{:S(2)}, u32[]{:S(2)}) %all-to-all-start.1) | async-done | bytes 4194336 | tf_op jit(solution)/shard_map/all_to_all | solution.py:462
  187.3 3.5 %combine.1 = bf16[64,2048]{1,0:T(8,128)(2,1)} custom-call(bf16[128,1024]{1,0:T(8,128)(2,1)} %pad_maximum_fusion.mix_ref, bf16[64,2048]{1,0:T(8,128)(2,1)} %add_convert_fusion.middle_ref, bf16[1024,2048]{1,0:T(8,128)(2,1)} %bitcast.36.returned_ref), custom_call_target="tpu_custom_call" | custom-call | flops 536870912 | bytes 4194304 | tf_op jit(solution)/shard_map/combine/pallas_call | solution.py:345
  (16 shorter events, 0.1 us)
Async XLA Ops:
  1.9 19.6 %copy-start.3 = (s32[64,8]{0,1:T(8,128)S(1)}, s32[64,8]{0,1:T(8,128)}, u32[]{:S(2)}) copy-start(s32[64,8]{0,1:T(8,128)} %param.31) | copy-start | bytes 6148
  1.9 19.9 %copy-start.2 = (bf16[64,64]{1,0:T(8,128)(2,1)S(1)}, bf16[64,64]{1,0:T(8,128)(2,1)}, u32[]{:S(2)}) copy-start(bf16[64,64]{1,0:T(8,128)(2,1)} %constant.41.clone) | copy-start | bytes 24580
  8.0 14.2 %copy-start.6 = (bf16[64,2048]{1,0:T(8,128)(2,1)S(1)}, bf16[64,2048]{1,0:T(8,128)(2,1)}, u32[]{:S(2)}) copy-start(bf16[64,2048]{1,0:T(8,128)(2,1)} %get-tuple-element.11) | copy-start | bytes 786436
  8.1 22.9 %collective-permute-start = (bf16[64,2048]{1,0:T(8,128)(2,1)}, bf16[64,2048]{1,0:T(8,128)(2,1)S(1)}, u32[]{:S(2)}, u32[]{:S(2)}) collective-permute-start(bf16[64,2048]{1,0:T(8,128)(2,1)} %get-tuple-element.11), channel_id=1, source_target_pairs={{0,96},{32,0},{64,32},{96,64},{1,97},{33,1},{65,33},{97,65},{2,98}... | collective-permute-start | bytes 786440 | tf_op jit(solution)/shard_map/ppermute | solution.py:385
  11.7 16.7 %collective-permute-start.7 = (bf16[64,2048]{1,0:T(8,128)(2,1)}, bf16[64,2048]{1,0:T(8,128)(2,1)S(1)}, u32[]{:S(2)}, u32[]{:S(2)}) collective-permute-start(bf16[64,2048]{1,0:T(8,128)(2,1)} %get-tuple-element.11), channel_id=1, source_target_pairs={{0,32},{32,64},{64,96},{96,0},{1,33},{33,65},{65,97},{97,1},{2,34}... | collective-permute-start | bytes 786440 | tf_op jit(solution)/shard_map/ppermute | solution.py:385
  16.6 9.7 %collective-permute-start.4 = (bf16[64,2048]{1,0:T(8,128)(2,1)}, bf16[64,2048]{1,0:T(8,128)(2,1)S(1)}, u32[]{:S(2)}, u32[]{:S(2)}) collective-permute-start(bf16[64,2048]{1,0:T(8,128)(2,1)} %get-tuple-element.15), channel_id=1, source_target_pairs={{0,32},{32,64},{64,96},{96,0},{1,33},{33,65},{65,97},{97,1},{2,34}... | collective-permute-start | bytes 786440 | tf_op jit(solution)/shard_map/ppermute | solution.py:385
  16.6 13.8 %collective-permute-start.1 = (bf16[64,2048]{1,0:T(8,128)(2,1)}, bf16[64,2048]{1,0:T(8,128)(2,1)S(1)}, u32[]{:S(2)}, u32[]{:S(2)}) collective-permute-start(bf16[64,2048]{1,0:T(8,128)(2,1)} %get-tuple-element.15), channel_id=1, source_target_pairs={{0,96},{32,0},{64,32},{96,64},{1,97},{33,1},{65,33},{97,65},{2,98}... | collective-permute-start | bytes 786440 | tf_op jit(solution)/shard_map/ppermute | solution.py:385
  22.2 6.2 %copy-start.5 = (bf16[4096,512]{1,0:T(8,128)(2,1)S(1)}, bf16[4096,512]{1,0:T(8,128)(2,1)}, u32[]{:S(2)}) copy-start(bf16[4096,512]{1,0:T(8,128)(2,1)} %param.29) | copy-start | bytes 12582916
  28.9 12.3 %collective-permute-start.8 = (bf16[64,512]{1,0:T(8,128)(2,1)S(1)}, bf16[64,512]{1,0:T(8,128)(2,1)S(1)}, u32[]{:S(2)}, u32[]{:S(2)}) collective-permute-start(bf16[64,512]{1,0:T(8,128)(2,1)S(1)} %fusion.31), channel_id=1, source_target_pairs={{0,96},{32,0},{64,32},{96,64},{1,97},{33,1},{65,33},{97,65},{2,98}... | collective-permute-start | bytes 196616 | tf_op jit(solution)/shard_map/ppermute | solution.py:385
  29.0 7.0 %collective-permute-start.5 = (bf16[64,2048]{1,0:T(8,128)(2,1)S(1)}, bf16[64,2048]{1,0:T(8,128)(2,1)S(1)}, u32[]{:S(2)}, u32[]{:S(2)}) collective-permute-start(bf16[64,2048]{1,0:T(8,128)(2,1)S(1)} %collective-permute-done.4), channel_id=1, source_target_pairs={{0,32},{32,64},{64,96},{96,0},{1,33},{33,65},{65,97},{97,1},{2,34}... | collective-permute-start | bytes 786440 | tf_op jit(solution)/shard_map/ppermute | solution.py:385
  30.9 12.2 %copy-start.1 = (bf16[64,2048]{1,0:T(8,128)(2,1)S(1)}, bf16[64,2048]{1,0:T(8,128)(2,1)}, u32[]{:S(2)}) copy-start(bf16[64,2048]{1,0:T(8,128)(2,1)} %param.19) | copy-start | bytes 786436
  31.4 9.8 %collective-permute-start.2 = (bf16[64,512]{1,0:T(8,128)(2,1)S(1)}, bf16[64,512]{1,0:T(8,128)(2,1)S(1)}, u32[]{:S(2)}, u32[]{:S(2)}) collective-permute-start(bf16[64,512]{1,0:T(8,128)(2,1)S(1)} %fusion.37), channel_id=1, source_target_pairs={{0,32},{32,64},{64,96},{96,0},{1,33},{33,65},{65,97},{97,1},{2,34}... | collective-permute-start | bytes 196616 | tf_op jit(solution)/shard_map/ppermute | solution.py:385
  31.5 6.4 %collective-permute-start.3 = (bf16[64,2048]{1,0:T(8,128)(2,1)S(1)}, bf16[64,2048]{1,0:T(8,128)(2,1)S(1)}, u32[]{:S(2)}, u32[]{:S(2)}) collective-permute-start(bf16[64,2048]{1,0:T(8,128)(2,1)S(1)} %collective-permute-done), channel_id=1, source_target_pairs={{0,96},{32,0},{64,32},{96,64},{1,97},{33,1},{65,33},{97,65},{2,98}... | collective-permute-start | bytes 786440 | tf_op jit(solution)/shard_map/ppermute | solution.py:385
  38.3 4.7 %collective-permute-start.6 = (bf16[64,512]{1,0:T(8,128)(2,1)S(1)}, bf16[64,512]{1,0:T(8,128)(2,1)S(1)}, u32[]{:S(2)}, u32[]{:S(2)}) collective-permute-start(bf16[64,512]{1,0:T(8,128)(2,1)S(1)} %fusion.34), channel_id=1, source_target_pairs={{0,64},{32,96},{64,0},{96,32},{1,65},{33,97},{65,1},{97,33},{2,66}... | collective-permute-start | bytes 196616 | tf_op jit(solution)/shard_map/ppermute | solution.py:385
  47.4 67.5 %copy-start = (bf16[1,2048,768]{2,1,0:T(8,128)(2,1)S(1)}, bf16[1,2048,768]{2,1,0:T(8,128)(2,1)}, u32[]{:S(2)}) copy-start(bf16[1,2048,768]{2,1,0:T(8,128)(2,1)} %param.33) | copy-start | bytes 9437188
  129.1 58.3 %all-to-all-start.1 = ((bf16[128,8,2048]{2,1,0:T(8,128)(2,1)}), bf16[128,8,2048]{2,1,0:T(8,128)(2,1)}, u32[]{:S(2)}, u32[]{:S(2)}) async-start(bf16[128,8,2048]{2,1,0:T(8,128)(2,1)} %bitcast.81), calls=%async_computation.1 | async-start | bytes 8388608 | tf_op jit(solution)/shard_map/all_to_all | solution.py:462
  134.6 4.4 %copy-start.4 = (f32[64,8]{0,1:T(8,128)S(1)}, f32[64,8]{0,1:T(8,128)}, u32[]{:S(2)}) copy-start(f32[64,8]{0,1:T(8,128)} %param.32) | copy-start | bytes 6148

commit v3 on v2

--- a/solution.py
+++ b/solution.py
@@ -432,20 +432,31 @@
     pick, mix = gather_plan(slots, route_gates, slot_count)
 
     inner = left.shape[1]
+    cut = inner // 2
+    rights = (right[:, :cut], right[:, cut:])
     up_left, down_left = shift(left, -1, req_size), shift(left, 1, req_size)
-    up_right, down_right = shift(right, -1, req_size), shift(right, 1, req_size)
+    up_rights, down_rights = [], []
+    for x in rights:
+        down_rights.append(shift(x, 1, req_size))
+        up_rights.append(shift(x, -1, req_size))
     far_left = shift(up_left, -1, req_size)
-    far_right = shift(down_right, 1, req_size)
+    far_rights = []
+    for x in down_rights:
+        far_rights.append(shift(x, 1, req_size))
 
     def project(a, b):
-        return (matmul(a, o_weight[:inner]) + matmul(b, o_weight[inner:])).astype(BF16)
-
-    own = project(left, right)
-    near_up = project(up_left, up_right)
-    near_down = project(down_left, down_right)
+        product = matmul(a, o_weight[:inner])
+        for i, x in enumerate(b):
+            product = product + matmul(x, o_weight[inner + i * cut : inner + (i + 1) * cut])
+        return product.astype(BF16)
+
+    own = matmul(left, o_weight[:inner]) + matmul(right, o_weight[inner:])
+    own = own.astype(BF16)
+    near_up = project(up_left, up_rights)
+    near_down = project(down_left, down_rights)
     from_up = shift(near_up, 1, req_size)
     from_down = shift(near_down, -1, req_size)
-    from_far = shift(project(far_left, far_right), 2, req_size)
+    from_far = shift(project(far_left, far_rights), 2, req_size)
     pieces = [own, from_down, from_far, from_up]
     at = lax.axis_index("req").astype(jnp.int32)
     columns = []

time: 191 us -> 199 us (1.042)
  starting transfers between devices: 17.9 us -> 22.7 us
  matrix products: 8.92 us -> 12.4 us
  waiting for transfers between devices: 54.1 us -> 51.4 us
    ppermute x9 -> x12, starting transfers between devices: 12.3 us -> 17.2 us  [shift(): return lax.ppermute(x, 'req', [(i, (i + by) % size) for i in range(size)])]
    dot_general x9 -> x12, matrix products: 8.92 us -> 12.4 us  [matmul(): return jnp.dot(a, b, preferred_element_type=F32)]
    ppermute x9 -> x12, waiting for transfers between devices: 6.86 us -> 4.16 us  [shift(): return lax.ppermute(x, 'req', [(i, (i + by) % size) for i in range(size)])]
  transfers between devices with their start and end apart: 10 -> 13, of which waited for: 5 -> 3; matrix products, arithmetic and copies ran while one was open for 6% -> 8% of each run, Pallas kernels for 5% -> 5%
where the time goes in v3:
time: 199 us; the launch traced here: 198 us
  blocking collectives  68.2 us (34%)
  waiting for transfers between devices  51.4 us (26%)
  Pallas kernels  36.6 us (18%)
  starting transfers between devices  22.7 us (11%)
  matrix products  12.4 us (6%)
  other arithmetic  3.49 us (2%)
  between operations  2.24 us (1%)
    all_to_all x1, blocking collectives, swap(): lax.all_to_all(x.reshape(expert_count, capacity, model_width), ('req', 'e...  68.2 us
    all_to_all x1, waiting for transfers between devices, swap(): lax.all_to_all(x.reshape(expert_count, capacity, model_width), ('req', 'e...  47.2 us
    ppermute x12, starting transfers between devices, shift(): return lax.ppermute(x, 'req', [(i, (i + by) % size) for i in range(size)])  17.2 us
    pallas_call x1, Pallas kernels, experts(): pl.pallas_call(functools.partial(experts_kernel, count), in_specs=[pl.Blo...  14.1 us
    dot_general x12, matrix products, matmul(): return jnp.dot(a, b, preferred_element_type=F32)  12.4 us
    pallas_call x2, Pallas kernels, attention(): pl.pallas_call(functools.partial(attention_kernel, made is None, span), g...  11 us
    all_to_all x1, starting transfers between devices, swap(): lax.all_to_all(x.reshape(expert_count, capacity, model_width), ('req', 'e...  5.53 us
    pallas_call x2, Pallas kernels, append(): pl.pallas_call(append_kernel, grid=(2,), in_specs=[pl.BlockSpec(memory_sp...  4.37 us
  transfers between devices with their start and end apart: 13, of which 3 were waited for; matrix products, arithmetic and copies ran while one was open for 8% of the time, Pallas kernels for 5%

profile of v3, /device:TPU:1, one launch (start us, length us, event | category | flops | bytes accessed | tf_op | source)
XLA Modules:
  0.0 198.2 jit_solution(14225574552234227759)
XLA Ops:
  1.9 6.1 %shard_map.202 = (bf16[64,2048]{1,0:T(8,128)(2,1)}, bf16[64,256]{1,0:T(8,128)(2,1)}, f32[64,128]{1,0:T(8,128)}, f32[64,128]{1,0:T(8,128)}, f32[64,128]{1,0:T(8,128)}, /*index=5*/bf16[80,64]{1,0:T(8,128)(2,1)}) custom-call(s32[1]{0:T(128)S(6)} %copy.31.refs_0_.length_ref, s32[1]{0:T(128)S(6)} %copy.32.refs_1_, f32[1,128]{1,0:T(1,128)} %bitcast.90, ...), custom_call_target="tpu_custom_call" | custom-call | flops 402653184 | bytes 2097152 | tf_op jit(solution)/shard_map/pallas_call | solution.py:181
  8.0 0.0 copy-start.6
  8.0 3.6 %collective-permute-start = (bf16[64,2048]{1,0:T(8,128)(2,1)}, bf16[64,2048]{1,0:T(8,128)(2,1)S(1)}, u32[]{:S(2)}, u32[]{:S(2)}) collective-permute-start(bf16[64,2048]{1,0:T(8,128)(2,1)} %get-tuple-element.11), channel_id=1, source_target_pairs={{0,96},{32,0},{64,32},{96,64},{1,97},{33,1},{65,33},{97,65},{2,98}... | collective-permute-start | bytes 786440 | tf_op jit(solution)/shard_map/ppermute | solution.py:385
  11.7 4.9 %shard_map.203 = (bf16[64,2048]{1,0:T(8,128)(2,1)}, bf16[64,256]{1,0:T(8,128)(2,1)}) custom-call(s32[1]{0:T(128)S(6)} %copy.31.refs_0_.length_ref, s32[1]{0:T(128)S(6)} %copy.32.refs_1_, f32[1,128]{1,0:T(1,128)} %bitcast.91, f32[1,128]{1,0:T(1,128)} %bitcast.93, bf16[64,4096]{1,0:T(8,128)(2,1)} %refs_4_.3, bf16[64,1024]{1,0:T(8,128)(2,1)} %rest_0_.1, ...), custom_call_target="tpu_custom_call" | custom-call | flops 402653184 | bytes 2097152 | tf_op jit(solution)/shard_map/pallas_call | solution.py:181
  16.6 1.0 fusion.65
  17.6 0.1 collective-permute-start.7
  17.7 2.7 %collective-permute-start.2 = (bf16[64,1024]{1,0:T(8,128)(2,1)S(1)}, bf16[64,1024]{1,0:T(8,128)(2,1)S(1)}, u32[]{:S(2)}, u32[]{:S(2)}) collective-permute-start(bf16[64,1024]{1,0:T(8,128)(2,1)S(1)} %get-tuple-element.24), channel_id=1, source_target_pairs={{0,96},{32,0},{64,32},{96,64},{1,97},{33,1},{65,33},{97,65},{2,98}... | collective-permute-start | bytes 393224 | tf_op jit(solution)/shard_map/ppermute | solution.py:385
  20.4 0.0 collective-permute-start.5
  20.4 2.2 %fusion = f32[64,512]{1,0:T(8,128)S(1)} fusion(bf16[64,2048]{1,0:T(8,128)(2,1)} %get-tuple-element.15, bf16[4096,512]{1,0:T(8,128)(2,1)} %param.29), kind=kOutput, calls=%fused_computation | convolution fusion | flops 134217728 | bytes 2490368 | tf_op jit(solution)/shard_map/dot_general | solution.py:26
  22.6 2.1 %fusion.31 = bf16[64,512]{1,0:T(8,128)(2,1)S(1)} fusion(f32[64,512]{1,0:T(8,128)S(1)} %fusion, bf16[64,2048]{1,0:T(8,128)(2,1)S(1)} %copy-done.6, bf16[4096,512]{1,0:T(8,128)(2,1)} %param.29), kind=kOutput, calls=%fused_computation.17 | convolution fusion | flops 134283264 | bytes 2555904 | tf_op jit(solution)/shard_map/dot_general | solution.py:26
  24.7 0.1 copy.29
  24.8 0.2 fusion.64
  24.9 0.1 fusion.66
  25.1 0.2 select_reduce_fusion
  25.3 0.1 copy.30
  25.4 2.7 %collective-permute-start.1 = (bf16[64,1024]{1,0:T(8,128)(2,1)S(1)}, bf16[64,1024]{1,0:T(8,128)(2,1)S(1)}, u32[]{:S(2)}, u32[]{:S(2)}) collective-permute-start(bf16[64,1024]{1,0:T(8,128)(2,1)S(1)} %get-tuple-element.23), channel_id=1, source_target_pairs={{0,96},{32,0},{64,32},{96,64},{1,97},{33,1},{65,33},{97,65},{2,98}... | collective-permute-start | bytes 393224 | tf_op jit(solution)/shard_map/ppermute | solution.py:385
  28.1 1.5 fusion.43
  29.7 0.1 collective-permute-start.8
  29.8 1.5 fusion.49
  31.3 0.1 collective-permute-start.6
  31.4 1.5 fusion.47
  32.9 1.5 fusion.53
  34.5 0.5 fusion.34
  34.9 0.0 copy-start.2
  35.0 2.7 %collective-permute-start.11 = (bf16[64,512]{1,0:T(8,128)(2,1)S(1)}, bf16[64,512]{1,0:T(8,128)(2,1)S(1)}, u32[]{:S(2)}, u32[]{:S(2)}) collective-permute-start(bf16[64,512]{1,0:T(8,128)(2,1)S(1)} %fusion.34), channel_id=1, source_target_pairs={{0,96},{32,0},{64,32},{96,64},{1,97},{33,1},{65,33},{97,65},{2,98}... | collective-permute-start | bytes 196616 | tf_op jit(solution)/shard_map/ppermute | solution.py:385
  37.7 0.5 fusion.40
  38.2 0.1 collective-permute-start.3
  38.3 2.7 %collective-permute-start.4 = (bf16[64,2048]{1,0:T(8,128)(2,1)S(1)}, bf16[64,2048]{1,0:T(8,128)(2,1)S(1)}, u32[]{:S(2)}, u32[]{:S(2)}) collective-permute-start(bf16[64,2048]{1,0:T(8,128)(2,1)S(1)} %collective-permute-done), channel_id=1, source_target_pairs={{0,96},{32,0},{64,32},{96,64},{1,97},{33,1},{65,33},{97,65},{2,98}... | collective-permute-start | bytes 786440 | tf_op jit(solution)/shard_map/ppermute | solution.py:385
  40.9 0.3 fusion.45
  41.2 0.3 fusion.51
  41.5 3.0 %collective-permute-done.4 = bf16[64,2048]{1,0:T(8,128)(2,1)S(1)} collective-permute-done((bf16[64,2048]{1,0:T(8,128)(2,1)S(1)}, bf16[64,2048]{1,0:T(8,128)(2,1)S(1)}, u32[]{:S(2)}, u32[]{:S(2)}) %collective-permute-start.4) | collective-permute-done | bytes 262176 | tf_op jit(solution)/shard_map/ppermute | solution.py:385
  44.5 0.5 fusion.37
  45.0 2.4 %collective-permute-start.9 = (bf16[64,512]{1,0:T(8,128)(2,1)S(1)}, bf16[64,512]{1,0:T(8,128)(2,1)S(1)}, u32[]{:S(2)}, u32[]{:S(2)}) collective-permute-start(bf16[64,512]{1,0:T(8,128)(2,1)S(1)} %fusion.37), channel_id=1, source_target_pairs={{0,64},{32,96},{64,0},{96,32},{1,65},{33,97},{65,1},{97,33},{2,66}... | collective-permute-start | bytes 196616 | tf_op jit(solution)/shard_map/ppermute | solution.py:385
  47.4 1.2 fusion.62.pick_ref
  48.5 1.2 collective-permute-done.9
  49.7 0.8 add_convert_fusion.middle_ref
  50.5 3.6 %outbox.1 = bf16[1024,2048]{1,0:T(8,128)(2,1)} custom-call(bf16[1024,64]{1,0:T(8,128)(2,1)} %fusion.62.pick_ref, bf16[64,2048]{1,0:T(8,128)(2,1)} %add_convert_fusion.middle_ref, f32[1,2048]{1,0:T(1,128)} %bitcast.89), custom_call_target="tpu_custom_call" | custom-call | flops 268435456 | bytes 4194304 | tf_op jit(solution)/shard_map/outbox/pallas_call | solution.py:255
  54.1 0.0 copy-start
  54.2 68.2 %all_to_all.10 = bf16[128,8,2048]{2,1,0:T(8,128)(2,1)} all-to-all(bf16[128,8,2048]{2,1,0:T(8,128)(2,1)} %bitcast.77), channel_id=1, replica_groups=mesh['req'=4,'exp'=32] {'req','exp'}, dimensions={0} | all-to-all | bytes 8388608 | tf_op jit(solution)/shard_map/all_to_all | solution.py:473
  122.4 14.1 %experts.1 = bf16[1024,2048]{1,0:T(8,128)(2,1)} custom-call(bf16[1024,2048]{1,0:T(8,128)(2,1)} %bitcast.85, bf16[2048,768]{1,0:T(8,128)(2,1)S(1)} %bitcast.76, bf16[2048,768]{1,0:T(8,128)(2,1)} %bitcast.94, bf16[768,2048]{1,0:T(8,128)(2,1)} %bitcast.95), custom_call_target="tpu_custom_call" | custom-call | flops 9663676416 | bytes 17825792 | tf_op jit(solution)/shard_map/experts/pallas_call | solution.py:317
  136.5 5.5 %all-to-all-start.1 = ((bf16[128,8,2048]{2,1,0:T(8,128)(2,1)}), bf16[128,8,2048]{2,1,0:T(8,128)(2,1)}, u32[]{:S(2)}, u32[]{:S(2)}) async-start(bf16[128,8,2048]{2,1,0:T(8,128)(2,1)} %bitcast.84), calls=%async_computation.1 | async-start | bytes 8388608 | tf_op jit(solution)/shard_map/all_to_all | solution.py:473
  142.0 0.0 copy-start.5
  142.0 2.2 %shard_map.205 = bf16[1024,512]{1,0:T(8,128)(2,1)} custom-call(s32[1]{0:T(128)S(6)} %copy.31.refs_0_.length_ref, bf16[80,64]{1,0:T(8,128)(2,1)} %get-tuple-element.16.place_ref, bf16[1024,512]{1,0:T(8,128)(2,1)} %bitcast.80, bf16[64,1024]{1,0:T(8,128)(2,1)} %rest_0_.1), custom_call_target="tpu_custom_call" | custom-call | flops 5242880 | bytes 2097152 | tf_op jit(solution)/shard_map/pallas_call | solution.py:218
  144.2 2.2 %shard_map.204 = bf16[1024,512]{1,0:T(8,128)(2,1)} custom-call(s32[1]{0:T(128)S(6)} %copy.31.refs_0_.length_ref, bf16[80,64]{1,0:T(8,128)(2,1)} %get-tuple-element.16.place_ref, bf16[1024,512]{1,0:T(8,128)(2,1)} %bitcast.83, bf16[64,256]{1,0:T(8,128)(2,1)} %get-tuple-element.17.rest_0_, bf16[64,256]{1,0:T(8,128)(2,1)} %get-tuple-element.18.rest_1_), custom_call_target="tpu_custom_call" | custom-call | flops 5242880 | bytes 2097152 | tf_op jit(solution)/shard_map/pallas_call | solution.py:218
  146.4 0.4 reduce-precision_convert_fusion
  146.8 0.7 pad_maximum_fusion.mix_ref
  147.5 47.2 %all-to-all-done.1 = bf16[128,8,2048]{2,1,0:T(8,128)(2,1)} async-done(((bf16[128,8,2048]{2,1,0:T(8,128)(2,1)}), bf16[128,8,2048]{2,1,0:T(8,128)(2,1)}, u32[]{:S(2)}, u32[]{:S(2)}) %all-to-all-start.1) | async-done | bytes 4194336 | tf_op jit(solution)/shard_map/all_to_all | solution.py:473
  194.7 3.5 %combine.1 = bf16[64,2048]{1,0:T(8,128)(2,1)} custom-call(bf16[128,1024]{1,0:T(8,128)(2,1)} %pad_maximum_fusion.mix_ref, bf16[64,2048]{1,0:T(8,128)(2,1)} %add_convert_fusion.middle_ref, bf16[1024,2048]{1,0:T(8,128)(2,1)} %bitcast.36.returned_ref), custom_call_target="tpu_custom_call" | custom-call | flops 536870912 | bytes 4194304 | tf_op jit(solution)/shard_map/combine/pallas_call | solution.py:345
  (26 shorter events, 0.1 us)
Async XLA Ops:
  8.0 14.6 %copy-start.6 = (bf16[64,2048]{1,0:T(8,128)(2,1)S(1)}, bf16[64,2048]{1,0:T(8,128)(2,1)}, u32[]{:S(2)}) copy-start(bf16[64,2048]{1,0:T(8,128)(2,1)} %get-tuple-element.11) | copy-start | bytes 786436
  8.0 29.7 %collective-permute-start = (bf16[64,2048]{1,0:T(8,128)(2,1)}, bf16[64,2048]{1,0:T(8,128)(2,1)S(1)}, u32[]{:S(2)}, u32[]{:S(2)}) collective-permute-start(bf16[64,2048]{1,0:T(8,128)(2,1)} %get-tuple-element.11), channel_id=1, source_target_pairs={{0,96},{32,0},{64,32},{96,64},{1,97},{33,1},{65,33},{97,65},{2,98}... | collective-permute-start | bytes 786440 | tf_op jit(solution)/shard_map/ppermute | solution.py:385
  11.6 22.8 %collective-permute-start.10 = (bf16[64,2048]{1,0:T(8,128)(2,1)}, bf16[64,2048]{1,0:T(8,128)(2,1)S(1)}, u32[]{:S(2)}, u32[]{:S(2)}) collective-permute-start(bf16[64,2048]{1,0:T(8,128)(2,1)} %get-tuple-element.11), channel_id=1, source_target_pairs={{0,32},{32,64},{64,96},{96,0},{1,33},{33,65},{65,97},{97,1},{2,34}... | collective-permute-start | bytes 786440 | tf_op jit(solution)/shard_map/ppermute | solution.py:385
  11.6 13.0 %copy-start.4 = (s32[64,8]{0,1:T(8,128)S(1)}, s32[64,8]{0,1:T(8,128)}, u32[]{:S(2)}) copy-start(s32[64,8]{0,1:T(8,128)} %param.31) | copy-start | bytes 6148
  11.7 13.3 %copy-start.3 = (bf16[64,64]{1,0:T(8,128)(2,1)S(1)}, bf16[64,64]{1,0:T(8,128)(2,1)}, u32[]{:S(2)}) copy-start(bf16[64,64]{1,0:T(8,128)(2,1)} %constant.41.clone) | copy-start | bytes 24580
  17.6 7.8 %collective-permute-start.7 = (bf16[64,1024]{1,0:T(8,128)(2,1)S(1)}, bf16[64,1024]{1,0:T(8,128)(2,1)S(1)}, u32[]{:S(2)}, u32[]{:S(2)}) collective-permute-start(bf16[64,1024]{1,0:T(8,128)(2,1)S(1)} %get-tuple-element.24), channel_id=1, source_target_pairs={{0,32},{32,64},{64,96},{96,0},{1,33},{33,65},{65,97},{97,1},{2,34}... | collective-permute-start | bytes 393224 | tf_op jit(solution)/shard_map/ppermute | solution.py:385
  17.7 13.6 %collective-permute-start.2 = (bf16[64,1024]{1,0:T(8,128)(2,1)S(1)}, bf16[64,1024]{1,0:T(8,128)(2,1)S(1)}, u32[]{:S(2)}, u32[]{:S(2)}) collective-permute-start(bf16[64,1024]{1,0:T(8,128)(2,1)S(1)} %get-tuple-element.24), channel_id=1, source_target_pairs={{0,96},{32,0},{64,32},{96,64},{1,97},{33,1},{65,33},{97,65},{2,98}... | collective-permute-start | bytes 393224 | tf_op jit(solution)/shard_map/ppermute | solution.py:385
  20.4 9.3 %collective-permute-start.5 = (bf16[64,1024]{1,0:T(8,128)(2,1)S(1)}, bf16[64,1024]{1,0:T(8,128)(2,1)S(1)}, u32[]{:S(2)}, u32[]{:S(2)}) collective-permute-start(bf16[64,1024]{1,0:T(8,128)(2,1)S(1)} %get-tuple-element.23), channel_id=1, source_target_pairs={{0,32},{32,64},{64,96},{96,0},{1,33},{33,65},{65,97},{97,1},{2,34}... | collective-permute-start | bytes 393224 | tf_op jit(solution)/shard_map/ppermute | solution.py:385
  25.4 9.1 %copy-start.1 = (bf16[4096,512]{1,0:T(8,128)(2,1)S(1)}, bf16[4096,512]{1,0:T(8,128)(2,1)}, u32[]{:S(2)}) copy-start(bf16[4096,512]{1,0:T(8,128)(2,1)} %param.29) | copy-start | bytes 12582916
  25.4 7.5 %collective-permute-start.1 = (bf16[64,1024]{1,0:T(8,128)(2,1)S(1)}, bf16[64,1024]{1,0:T(8,128)(2,1)S(1)}, u32[]{:S(2)}, u32[]{:S(2)}) collective-permute-start(bf16[64,1024]{1,0:T(8,128)(2,1)S(1)} %get-tuple-element.23), channel_id=1, source_target_pairs={{0,96},{32,0},{64,32},{96,64},{1,97},{33,1},{65,33},{97,65},{2,98}... | collective-permute-start | bytes 393224 | tf_op jit(solution)/shard_map/ppermute | solution.py:385
  29.7 11.2 %collective-permute-start.8 = (bf16[64,1024]{1,0:T(8,128)(2,1)S(1)}, bf16[64,1024]{1,0:T(8,128)(2,1)S(1)}, u32[]{:S(2)}, u32[]{:S(2)}) collective-permute-start(bf16[64,1024]{1,0:T(8,128)(2,1)S(1)} %collective-permute-done.7), channel_id=1, source_target_pairs={{0,32},{32,64},{64,96},{96,0},{1,33},{33,65},{65,97},{97,1},{2,34}... | collective-permute-start | bytes 393224 | tf_op jit(solution)/shard_map/ppermute | solution.py:385
  31.3 9.9 %collective-permute-start.6 = (bf16[64,1024]{1,0:T(8,128)(2,1)S(1)}, bf16[64,1024]{1,0:T(8,128)(2,1)S(1)}, u32[]{:S(2)}, u32[]{:S(2)}) collective-permute-start(bf16[64,1024]{1,0:T(8,128)(2,1)S(1)} %collective-permute-done.5), channel_id=1, source_target_pairs={{0,32},{32,64},{64,96},{96,0},{1,33},{33,65},{65,97},{97,1},{2,34}... | collective-permute-start | bytes 393224 | tf_op jit(solution)/shard_map/ppermute | solution.py:385
  34.9 14.8 %copy-start.2 = (bf16[64,2048]{1,0:T(8,128)(2,1)S(1)}, bf16[64,2048]{1,0:T(8,128)(2,1)}, u32[]{:S(2)}) copy-start(bf16[64,2048]{1,0:T(8,128)(2,1)} %param.19) | copy-start | bytes 786436
  35.0 13.6 %collective-permute-start.11 = (bf16[64,512]{1,0:T(8,128)(2,1)S(1)}, bf16[64,512]{1,0:T(8,128)(2,1)S(1)}, u32[]{:S(2)}, u32[]{:S(2)}) collective-permute-start(bf16[64,512]{1,0:T(8,128)(2,1)S(1)} %fusion.34), channel_id=1, source_target_pairs={{0,96},{32,0},{64,32},{96,64},{1,97},{33,1},{65,33},{97,65},{2,98}... | collective-permute-start | bytes 196616 | tf_op jit(solution)/shard_map/ppermute | solution.py:385
  38.2 10.4 %collective-permute-start.3 = (bf16[64,512]{1,0:T(8,128)(2,1)S(1)}, bf16[64,512]{1,0:T(8,128)(2,1)S(1)}, u32[]{:S(2)}, u32[]{:S(2)}) collective-permute-start(bf16[64,512]{1,0:T(8,128)(2,1)S(1)} %fusion.40), channel_id=1, source_target_pairs={{0,32},{32,64},{64,96},{96,0},{1,33},{33,65},{65,97},{97,1},{2,34}... | collective-permute-start | bytes 196616 | tf_op jit(solution)/shard_map/ppermute | solution.py:385
  38.3 6.3 %collective-permute-start.4 = (bf16[64,2048]{1,0:T(8,128)(2,1)S(1)}, bf16[64,2048]{1,0:T(8,128)(2,1)S(1)}, u32[]{:S(2)}, u32[]{:S(2)}) collective-permute-start(bf16[64,2048]{1,0:T(8,128)(2,1)S(1)} %collective-permute-done), channel_id=1, source_target_pairs={{0,96},{32,0},{64,32},{96,64},{1,97},{33,1},{65,33},{97,65},{2,98}... | collective-permute-start | bytes 786440 | tf_op jit(solution)/shard_map/ppermute | solution.py:385
  45.0 4.7 %collective-permute-start.9 = (bf16[64,512]{1,0:T(8,128)(2,1)S(1)}, bf16[64,512]{1,0:T(8,128)(2,1)S(1)}, u32[]{:S(2)}, u32[]{:S(2)}) collective-permute-start(bf16[64,512]{1,0:T(8,128)(2,1)S(1)} %fusion.37), channel_id=1, source_target_pairs={{0,64},{32,96},{64,0},{96,32},{1,65},{33,97},{65,1},{97,33},{2,66}... | collective-permute-start | bytes 196616 | tf_op jit(solution)/shard_map/ppermute | solution.py:385
  54.1 68.2 %copy-start = (bf16[1,2048,768]{2,1,0:T(8,128)(2,1)S(1)}, bf16[1,2048,768]{2,1,0:T(8,128)(2,1)}, u32[]{:S(2)}) copy-start(bf16[1,2048,768]{2,1,0:T(8,128)(2,1)} %param.33) | copy-start | bytes 9437188
  136.5 58.3 %all-to-all-start.1 = ((bf16[128,8,2048]{2,1,0:T(8,128)(2,1)}), bf16[128,8,2048]{2,1,0:T(8,128)(2,1)}, u32[]{:S(2)}, u32[]{:S(2)}) async-start(bf16[128,8,2048]{2,1,0:T(8,128)(2,1)} %bitcast.84), calls=%async_computation.1 | async-start | bytes 8388608 | tf_op jit(solution)/shard_map/all_to_all | solution.py:473
  142.0 4.4 %copy-start.5 = (f32[64,8]{0,1:T(8,128)S(1)}, f32[64,8]{0,1:T(8,128)}, u32[]{:S(2)}) copy-start(f32[64,8]{0,1:T(8,128)} %param.32) | copy-start | bytes 6148

commit v4 on v2

--- a/solution.py
+++ b/solution.py
@@ -251,7 +251,7 @@
 def outbox(pick, middle, gain):
     slots, tokens = pick.shape
     width = middle.shape[1]
-    count = 4
+    count = 8
     return pl.pallas_call(
         functools.partial(outbox_kernel, count),
         in_specs=[pl.BlockSpec(memory_space=pltpu.VMEM)] * 3,
@@ -287,6 +287,17 @@
     for each in [x_in[0], *weights_in[:3], *x_in[1:], weights_in[3]]:
         each.start()
     sent = []
+    held = []
+
+    def finish(i):
+        r = rows[i]
+        if i == 0:
+            weights_in[3].wait()
+        out_buf[r, :] = matmul(held[i], down_buf[...]).astype(BF16)
+        out = copy(out_buf.at[r], out_hbm.at[r], out_sems.at[i])
+        out.start()
+        sent.append(out)
+
     for i, r in enumerate(rows):
         x_in[i].wait()
         x = x_buf[r, :]
@@ -299,13 +310,10 @@
         else:
             gate = matmul(x, gate_buf[...])
         up = matmul(x, up_buf[...])
-        hidden = (gate / (1.0 + jnp.exp(-gate)) * up).astype(BF16)
-        if i == 0:
-            weights_in[3].wait()
-        out_buf[r, :] = matmul(hidden, down_buf[...]).astype(BF16)
-        out = copy(out_buf.at[r], out_hbm.at[r], out_sems.at[i])
-        out.start()
-        sent.append(out)
+        held.append((gate / (1.0 + jnp.exp(-gate)) * up).astype(BF16))
+        if i:
+            finish(i - 1)
+    finish(len(rows) - 1)
     for out in sent:
         out.wait()
 
@@ -321,7 +329,7 @@
         out_shape=jax.ShapeDtypeStruct(x.shape, BF16),
         scratch_shapes=[pltpu.VMEM(a.shape, BF16) for a in (x, w_gate, w_up, w_down, x)]
         + [pltpu.SemaphoreType.DMA((n,)) for n in (count, 4, count)],
-        compiler_params=pltpu.CompilerParams(vmem_limit_bytes=48 << 20),
+        compiler_params=pltpu.CompilerParams(vmem_limit_bytes=43 << 20),
         name="experts",
         cost_estimate=pl.CostEstimate(
             flops=6 * slots * width * inner,

time: 191 us -> 191 us (level)
  no operation moved by 1% of the time
where the time goes in v4:
time: 191 us
  blocking collectives  67.5 us (35%)
  waiting for transfers between devices  54 us (28%)
  Pallas kernels  36.5 us (19%)
  starting transfers between devices  17.9 us (9%)
  matrix products  8.92 us (5%)
  other arithmetic  3.48 us (2%)
  between operations  2.21 us (1%)
    all_to_all x1, blocking collectives, swap(): lax.all_to_all(x.reshape(expert_count, capacity, model_width), ('req', 'e...  67.5 us
    all_to_all x1, waiting for transfers between devices, swap(): lax.all_to_all(x.reshape(expert_count, capacity, model_width), ('req', 'e...  47.2 us
    pallas_call x1, Pallas kernels, experts(): pl.pallas_call(functools.partial(experts_kernel, count), in_specs=[pl.Blo...  13.9 us
    ppermute x9, starting transfers between devices, shift(): return lax.ppermute(x, 'req', [(i, (i + by) % size) for i in range(size)])  12.3 us
    pallas_call x2, Pallas kernels, attention(): pl.pallas_call(functools.partial(attention_kernel, made is None, span), g...  11 us
    dot_general x9, matrix products, matmul(): return jnp.dot(a, b, preferred_element_type=F32)  8.92 us
    ppermute x9, waiting for transfers between devices, shift(): return lax.ppermute(x, 'req', [(i, (i + by) % size) for i in range(size)])  6.86 us
    all_to_all x1, starting transfers between devices, swap(): lax.all_to_all(x.reshape(expert_count, capacity, model_width), ('req', 'e...  5.53 us
  transfers between devices with their start and end apart: 10, of which 5 were waited for; matrix products, arithmetic and copies ran while one was open for 6% of the time, Pallas kernels for 5%

profile of v4, /device:TPU:1, one launch (start us, length us, event | category | flops | bytes accessed | tf_op | source)
XLA Modules:
  0.0 190.7 jit_solution(17977354311119682627)
XLA Ops:
  1.9 0.0 copy-start.4
  1.9 6.1 %shard_map.202 = (bf16[64,2048]{1,0:T(8,128)(2,1)}, bf16[64,256]{1,0:T(8,128)(2,1)}, f32[64,128]{1,0:T(8,128)}, f32[64,128]{1,0:T(8,128)}, f32[64,128]{1,0:T(8,128)}, /*index=5*/bf16[80,64]{1,0:T(8,128)(2,1)}) custom-call(s32[1]{0:T(128)S(6)} %copy.31.refs_0_.length_ref, s32[1]{0:T(128)S(6)} %copy.32.refs_1_, f32[1,128]{1,0:T(1,128)} %bitcast.89, ...), custom_call_target="tpu_custom_call" | custom-call | flops 402653184 | bytes 2097152 | tf_op jit(solution)/shard_map/pallas_call | solution.py:181
  8.0 0.0 copy-start.8
  8.1 3.6 %collective-permute-start = (bf16[64,2048]{1,0:T(8,128)(2,1)}, bf16[64,2048]{1,0:T(8,128)(2,1)S(1)}, u32[]{:S(2)}, u32[]{:S(2)}) collective-permute-start(bf16[64,2048]{1,0:T(8,128)(2,1)} %get-tuple-element.11), channel_id=1, source_target_pairs={{0,96},{32,0},{64,32},{96,64},{1,97},{33,1},{65,33},{97,65},{2,98}... | collective-permute-start | bytes 786440 | tf_op jit(solution)/shard_map/ppermute | solution.py:393
  11.7 0.0 collective-permute-start.7
  11.7 4.9 %shard_map.203 = (bf16[64,2048]{1,0:T(8,128)(2,1)}, bf16[64,256]{1,0:T(8,128)(2,1)}) custom-call(s32[1]{0:T(128)S(6)} %copy.31.refs_0_.length_ref, s32[1]{0:T(128)S(6)} %copy.32.refs_1_, f32[1,128]{1,0:T(1,128)} %bitcast.90, f32[1,128]{1,0:T(1,128)} %bitcast.92, bf16[64,4096]{1,0:T(8,128)(2,1)} %refs_4_.3, bf16[64,1024]{1,0:T(8,128)(2,1)} %rest_0_.1, ...), custom_call_target="tpu_custom_call" | custom-call | flops 402653184 | bytes 2097152 | tf_op jit(solution)/shard_map/pallas_call | solution.py:181
  16.6 0.0 collective-permute-start.4
  16.6 2.7 %collective-permute-start.1 = (bf16[64,2048]{1,0:T(8,128)(2,1)}, bf16[64,2048]{1,0:T(8,128)(2,1)S(1)}, u32[]{:S(2)}, u32[]{:S(2)}) collective-permute-start(bf16[64,2048]{1,0:T(8,128)(2,1)} %get-tuple-element.15), channel_id=1, source_target_pairs={{0,96},{32,0},{64,32},{96,64},{1,97},{33,1},{65,33},{97,65},{2,98}... | collective-permute-start | bytes 786440 | tf_op jit(solution)/shard_map/ppermute | solution.py:393
  19.4 2.2 %fusion = f32[64,512]{1,0:T(8,128)S(1)} fusion(bf16[64,2048]{1,0:T(8,128)(2,1)} %get-tuple-element.15, bf16[4096,512]{1,0:T(8,128)(2,1)} %param.29), kind=kOutput, calls=%fused_computation | convolution fusion | flops 134217728 | bytes 2490368 | tf_op jit(solution)/shard_map/dot_general | solution.py:26
  21.5 0.1 copy.29
  21.6 0.2 fusion.49
  21.8 0.1 fusion.50
  21.9 0.2 select_reduce_fusion
  22.2 0.1 copy.30
  22.3 2.2 %fusion.28 = bf16[64,512]{1,0:T(8,128)(2,1)S(1)} fusion(f32[64,512]{1,0:T(8,128)S(1)} %fusion, bf16[64,2048]{1,0:T(8,128)(2,1)S(1)} %copy-done.8, bf16[4096,512]{1,0:T(8,128)(2,1)} %param.29), kind=kOutput, calls=%fused_computation.20 | convolution fusion | flops 134283264 | bytes 2555904 | tf_op jit(solution)/shard_map/dot_general | solution.py:26
  24.5 1.8 collective-permute-done.4
  26.3 2.1 %fusion.2 = f32[64,512]{1,0:T(8,128)S(1)} fusion(bf16[64,2048]{1,0:T(8,128)(2,1)S(1)} %collective-permute-done.4, bf16[4096,512]{1,0:T(8,128)(2,1)} %param.29), kind=kOutput, calls=%fused_computation.2 | convolution fusion | flops 134217728 | bytes 2490368 | tf_op jit(solution)/shard_map/dot_general | solution.py:26
  28.4 0.0 collective-permute-done.7
  28.4 0.5 fusion.31
  28.9 0.1 collective-permute-start.8
  29.0 1.5 collective-permute-start.5
  30.4 0.0 collective-permute-done.1
  30.4 0.5 fusion.6
  30.9 0.0 copy-start.3
  30.9 0.5 fusion.37
  31.4 0.1 collective-permute-start.2
  31.5 2.7 %collective-permute-start.3 = (bf16[64,2048]{1,0:T(8,128)(2,1)S(1)}, bf16[64,2048]{1,0:T(8,128)(2,1)S(1)}, u32[]{:S(2)}, u32[]{:S(2)}) collective-permute-start(bf16[64,2048]{1,0:T(8,128)(2,1)S(1)} %collective-permute-done), channel_id=1, source_target_pairs={{0,96},{32,0},{64,32},{96,64},{1,97},{33,1},{65,33},{97,65},{2,98}... | collective-permute-start | bytes 786440 | tf_op jit(solution)/shard_map/ppermute | solution.py:393
  34.1 1.9 collective-permute-done.5
  36.0 0.5 fusion.4
  36.5 1.4 collective-permute-done.3
  37.8 0.5 fusion.34
  38.3 1.7 collective-permute-start.6
  40.0 1.2 fusion.47.pick_ref
  41.2 1.8 collective-permute-done.6
  43.1 0.8 add_convert_fusion.middle_ref
  43.8 3.7 %outbox.1 = bf16[1024,2048]{1,0:T(8,128)(2,1)} custom-call(bf16[1024,64]{1,0:T(8,128)(2,1)} %fusion.47.pick_ref, bf16[64,2048]{1,0:T(8,128)(2,1)} %add_convert_fusion.middle_ref, f32[1,2048]{1,0:T(1,128)} %bitcast.88), custom_call_target="tpu_custom_call" | custom-call | flops 268435456 | bytes 4194304 | tf_op jit(solution)/shard_map/outbox/pallas_call | solution.py:255
  47.5 0.0 copy-start
  47.5 0.0 copy-start.1
  47.5 67.5 %all_to_all.10 = bf16[128,8,2048]{2,1,0:T(8,128)(2,1)} all-to-all(bf16[128,8,2048]{2,1,0:T(8,128)(2,1)} %bitcast.76), channel_id=1, replica_groups=mesh['req'=4,'exp'=32] {'req','exp'}, dimensions={0} | all-to-all | bytes 8388608 | tf_op jit(solution)/shard_map/all_to_all | solution.py:470
  115.0 13.9 %experts.1 = bf16[1024,2048]{1,0:T(8,128)(2,1)} custom-call(bf16[1024,2048]{1,0:T(8,128)(2,1)} %bitcast.84, bf16[2048,768]{1,0:T(8,128)(2,1)S(1)} %bitcast.73, bf16[2048,768]{1,0:T(8,128)(2,1)S(1)} %bitcast.74, bf16[768,2048]{1,0:T(8,128)(2,1)S(1)} %bitcast.75), custom_call_target="tpu_custom_call" | custom-call | flops 9663676416 | bytes 17825792 | tf_op jit(solution)/shard_map/experts/pallas_call | solution.py:325
  128.9 5.5 %all-to-all-start.1 = ((bf16[128,8,2048]{2,1,0:T(8,128)(2,1)}), bf16[128,8,2048]{2,1,0:T(8,128)(2,1)}, u32[]{:S(2)}, u32[]{:S(2)}) async-start(bf16[128,8,2048]{2,1,0:T(8,128)(2,1)} %bitcast.83), calls=%async_computation.1 | async-start | bytes 8388608 | tf_op jit(solution)/shard_map/all_to_all | solution.py:470
  134.4 0.0 copy-start.6
  134.5 2.2 %shard_map.205 = bf16[1024,512]{1,0:T(8,128)(2,1)} custom-call(s32[1]{0:T(128)S(6)} %copy.31.refs_0_.length_ref, bf16[80,64]{1,0:T(8,128)(2,1)} %get-tuple-element.16.place_ref, bf16[1024,512]{1,0:T(8,128)(2,1)} %bitcast.79, bf16[64,1024]{1,0:T(8,128)(2,1)} %rest_0_.1), custom_call_target="tpu_custom_call" | custom-call | flops 5242880 | bytes 2097152 | tf_op jit(solution)/shard_map/pallas_call | solution.py:218
  136.7 2.2 %shard_map.204 = bf16[1024,512]{1,0:T(8,128)(2,1)} custom-call(s32[1]{0:T(128)S(6)} %copy.31.refs_0_.length_ref, bf16[80,64]{1,0:T(8,128)(2,1)} %get-tuple-element.16.place_ref, bf16[1024,512]{1,0:T(8,128)(2,1)} %bitcast.82, bf16[64,256]{1,0:T(8,128)(2,1)} %get-tuple-element.17.rest_0_, bf16[64,256]{1,0:T(8,128)(2,1)} %get-tuple-element.18.rest_1_), custom_call_target="tpu_custom_call" | custom-call | flops 5242880 | bytes 2097152 | tf_op jit(solution)/shard_map/pallas_call | solution.py:218
  138.9 0.4 reduce-precision_convert_fusion
  139.2 0.7 pad_maximum_fusion.mix_ref
  140.0 47.2 %all-to-all-done.1 = bf16[128,8,2048]{2,1,0:T(8,128)(2,1)} async-done(((bf16[128,8,2048]{2,1,0:T(8,128)(2,1)}), bf16[128,8,2048]{2,1,0:T(8,128)(2,1)}, u32[]{:S(2)}, u32[]{:S(2)}) %all-to-all-start.1) | async-done | bytes 4194336 | tf_op jit(solution)/shard_map/all_to_all | solution.py:470
  187.2 3.5 %combine.1 = bf16[64,2048]{1,0:T(8,128)(2,1)} custom-call(bf16[128,1024]{1,0:T(8,128)(2,1)} %pad_maximum_fusion.mix_ref, bf16[64,2048]{1,0:T(8,128)(2,1)} %add_convert_fusion.middle_ref, bf16[1024,2048]{1,0:T(8,128)(2,1)} %bitcast.36.returned_ref), custom_call_target="tpu_custom_call" | custom-call | flops 536870912 | bytes 4194304 | tf_op jit(solution)/shard_map/combine/pallas_call | solution.py:353
  (20 shorter events, 0.1 us)
Async XLA Ops:
  1.9 19.6 %copy-start.5 = (s32[64,8]{0,1:T(8,128)S(1)}, s32[64,8]{0,1:T(8,128)}, u32[]{:S(2)}) copy-start(s32[64,8]{0,1:T(8,128)} %param.31) | copy-start | bytes 6148
  1.9 19.9 %copy-start.4 = (bf16[64,64]{1,0:T(8,128)(2,1)S(1)}, bf16[64,64]{1,0:T(8,128)(2,1)}, u32[]{:S(2)}) copy-start(bf16[64,64]{1,0:T(8,128)(2,1)} %constant.41.clone) | copy-start | bytes 24580
  8.0 14.2 %copy-start.8 = (bf16[64,2048]{1,0:T(8,128)(2,1)S(1)}, bf16[64,2048]{1,0:T(8,128)(2,1)}, u32[]{:S(2)}) copy-start(bf16[64,2048]{1,0:T(8,128)(2,1)} %get-tuple-element.11) | copy-start | bytes 786436
  8.1 22.9 %collective-permute-start = (bf16[64,2048]{1,0:T(8,128)(2,1)}, bf16[64,2048]{1,0:T(8,128)(2,1)S(1)}, u32[]{:S(2)}, u32[]{:S(2)}) collective-permute-start(bf16[64,2048]{1,0:T(8,128)(2,1)} %get-tuple-element.11), channel_id=1, source_target_pairs={{0,96},{32,0},{64,32},{96,64},{1,97},{33,1},{65,33},{97,65},{2,98}... | collective-permute-start | bytes 786440 | tf_op jit(solution)/shard_map/ppermute | solution.py:393
  11.7 16.7 %collective-permute-start.7 = (bf16[64,2048]{1,0:T(8,128)(2,1)}, bf16[64,2048]{1,0:T(8,128)(2,1)S(1)}, u32[]{:S(2)}, u32[]{:S(2)}) collective-permute-start(bf16[64,2048]{1,0:T(8,128)(2,1)} %get-tuple-element.11), channel_id=1, source_target_pairs={{0,32},{32,64},{64,96},{96,0},{1,33},{33,65},{65,97},{97,1},{2,34}... | collective-permute-start | bytes 786440 | tf_op jit(solution)/shard_map/ppermute | solution.py:393
  16.6 9.7 %collective-permute-start.4 = (bf16[64,2048]{1,0:T(8,128)(2,1)}, bf16[64,2048]{1,0:T(8,128)(2,1)S(1)}, u32[]{:S(2)}, u32[]{:S(2)}) collective-permute-start(bf16[64,2048]{1,0:T(8,128)(2,1)} %get-tuple-element.15), channel_id=1, source_target_pairs={{0,32},{32,64},{64,96},{96,0},{1,33},{33,65},{65,97},{97,1},{2,34}... | collective-permute-start | bytes 786440 | tf_op jit(solution)/shard_map/ppermute | solution.py:393
  16.6 13.8 %collective-permute-start.1 = (bf16[64,2048]{1,0:T(8,128)(2,1)}, bf16[64,2048]{1,0:T(8,128)(2,1)S(1)}, u32[]{:S(2)}, u32[]{:S(2)}) collective-permute-start(bf16[64,2048]{1,0:T(8,128)(2,1)} %get-tuple-element.15), channel_id=1, source_target_pairs={{0,96},{32,0},{64,32},{96,64},{1,97},{33,1},{65,33},{97,65},{2,98}... | collective-permute-start | bytes 786440 | tf_op jit(solution)/shard_map/ppermute | solution.py:393
  22.2 6.2 %copy-start.7 = (bf16[4096,512]{1,0:T(8,128)(2,1)S(1)}, bf16[4096,512]{1,0:T(8,128)(2,1)}, u32[]{:S(2)}) copy-start(bf16[4096,512]{1,0:T(8,128)(2,1)} %param.29) | copy-start | bytes 12582916
  28.9 12.3 %collective-permute-start.8 = (bf16[64,512]{1,0:T(8,128)(2,1)S(1)}, bf16[64,512]{1,0:T(8,128)(2,1)S(1)}, u32[]{:S(2)}, u32[]{:S(2)}) collective-permute-start(bf16[64,512]{1,0:T(8,128)(2,1)S(1)} %fusion.31), channel_id=1, source_target_pairs={{0,96},{32,0},{64,32},{96,64},{1,97},{33,1},{65,33},{97,65},{2,98}... | collective-permute-start | bytes 196616 | tf_op jit(solution)/shard_map/ppermute | solution.py:393
  29.0 7.0 %collective-permute-start.5 = (bf16[64,2048]{1,0:T(8,128)(2,1)S(1)}, bf16[64,2048]{1,0:T(8,128)(2,1)S(1)}, u32[]{:S(2)}, u32[]{:S(2)}) collective-permute-start(bf16[64,2048]{1,0:T(8,128)(2,1)S(1)} %collective-permute-done.4), channel_id=1, source_target_pairs={{0,32},{32,64},{64,96},{96,0},{1,33},{33,65},{65,97},{97,1},{2,34}... | collective-permute-start | bytes 786440 | tf_op jit(solution)/shard_map/ppermute | solution.py:393
  30.9 12.2 %copy-start.3 = (bf16[64,2048]{1,0:T(8,128)(2,1)S(1)}, bf16[64,2048]{1,0:T(8,128)(2,1)}, u32[]{:S(2)}) copy-start(bf16[64,2048]{1,0:T(8,128)(2,1)} %param.19) | copy-start | bytes 786436
  31.4 9.8 %collective-permute-start.2 = (bf16[64,512]{1,0:T(8,128)(2,1)S(1)}, bf16[64,512]{1,0:T(8,128)(2,1)S(1)}, u32[]{:S(2)}, u32[]{:S(2)}) collective-permute-start(bf16[64,512]{1,0:T(8,128)(2,1)S(1)} %fusion.37), channel_id=1, source_target_pairs={{0,32},{32,64},{64,96},{96,0},{1,33},{33,65},{65,97},{97,1},{2,34}... | collective-permute-start | bytes 196616 | tf_op jit(solution)/shard_map/ppermute | solution.py:393
  31.5 6.4 %collective-permute-start.3 = (bf16[64,2048]{1,0:T(8,128)(2,1)S(1)}, bf16[64,2048]{1,0:T(8,128)(2,1)S(1)}, u32[]{:S(2)}, u32[]{:S(2)}) collective-permute-start(bf16[64,2048]{1,0:T(8,128)(2,1)S(1)} %collective-permute-done), channel_id=1, source_target_pairs={{0,96},{32,0},{64,32},{96,64},{1,97},{33,1},{65,33},{97,65},{2,98}... | collective-permute-start | bytes 786440 | tf_op jit(solution)/shard_map/ppermute | solution.py:393
  38.3 4.7 %collective-permute-start.6 = (bf16[64,512]{1,0:T(8,128)(2,1)S(1)}, bf16[64,512]{1,0:T(8,128)(2,1)S(1)}, u32[]{:S(2)}, u32[]{:S(2)}) collective-permute-start(bf16[64,512]{1,0:T(8,128)(2,1)S(1)} %fusion.34), channel_id=1, source_target_pairs={{0,64},{32,96},{64,0},{96,32},{1,65},{33,97},{65,1},{97,33},{2,66}... | collective-permute-start | bytes 196616 | tf_op jit(solution)/shard_map/ppermute | solution.py:393
  43.8 71.2 %copy-start.2 = (bf16[1,768,2048]{2,1,0:T(8,128)(2,1)S(1)}, bf16[1,768,2048]{2,1,0:T(8,128)(2,1)}, u32[]{:S(2)}) copy-start(bf16[1,768,2048]{2,1,0:T(8,128)(2,1)} %param.35) | copy-start | bytes 9437188
  47.5 67.5 %copy-start = (bf16[1,2048,768]{2,1,0:T(8,128)(2,1)S(1)}, bf16[1,2048,768]{2,1,0:T(8,128)(2,1)}, u32[]{:S(2)}) copy-start(bf16[1,2048,768]{2,1,0:T(8,128)(2,1)} %param.33) | copy-start | bytes 9437188
  47.5 67.5 %copy-start.1 = (bf16[1,2048,768]{2,1,0:T(8,128)(2,1)S(1)}, bf16[1,2048,768]{2,1,0:T(8,128)(2,1)}, u32[]{:S(2)}) copy-start(bf16[1,2048,768]{2,1,0:T(8,128)(2,1)} %param.34) | copy-start | bytes 9437188
  128.9 58.3 %all-to-all-start.1 = ((bf16[128,8,2048]{2,1,0:T(8,128)(2,1)}), bf16[128,8,2048]{2,1,0:T(8,128)(2,1)}, u32[]{:S(2)}, u32[]{:S(2)}) async-start(bf16[128,8,2048]{2,1,0:T(8,128)(2,1)} %bitcast.83), calls=%async_computation.1 | async-start | bytes 8388608 | tf_op jit(solution)/shard_map/all_to_all | solution.py:470
  134.4 4.4 %copy-start.6 = (f32[64,8]{0,1:T(8,128)S(1)}, f32[64,8]{0,1:T(8,128)}, u32[]{:S(2)}) copy-start(f32[64,8]{0,1:T(8,128)} %param.32) | copy-start | bytes 6148
